TPU v7x, 32 devices: a whole 2x2x4 slice. The times are simulated.
32 devices in a mesh: fsdp: 8 (over y, x, core), tp: 4 (over z).
Axes of the slice: x: 2, y: 2, z: 4, core: 2. Of those that a mesh axis runs over, the one named last changes fastest.
Arguments:
- tokens: bfloat16 [8192, 2048], P(('fsdp', 'tp')), may hold values from -6 to 6
- segments: int32 [8, 1024], P('fsdp'), may hold values from 0 to 7, never falling along the last dimension, each value on 1 to 512 neighbouring positions
- prefix: int32 [8], P('fsdp'), may hold values from 0 to 512
- expert_ids: int32 [8192, 8], P('fsdp'), may hold values from 0 to 31, all different within a row
- first_gain: bfloat16 [2048], P('fsdp'), may hold values from 0.25 to 1.75
- query_weight: bfloat16 [2048, 4096], P('fsdp', 'tp'), may hold values from -0.125 to 0.125
- key_matrix: bfloat16 [2048, 512], P('fsdp', 'tp'), may hold values from -0.125 to 0.125
- value_matrix: bfloat16 [2048, 512], P('fsdp', 'tp'), may hold values from -0.125 to 0.125
- query_gain: bfloat16 [128], P('fsdp'), may hold values from 0.25 to 1.75
- key_gain: bfloat16 [128], P('fsdp'), may hold values from 0.25 to 1.75
- output_weight: bfloat16 [2048, 4096], P('fsdp', 'tp'), may hold values from -0.75 to 0.75
- second_gain: bfloat16 [2048], P('fsdp'), may hold values from 0.25 to 1.75
- router: bfloat16 [2048, 32], P('fsdp'), may hold values from -0.125 to 0.125
- gate_weight: bfloat16 [32, 768, 2048], P('fsdp', 'tp'), may hold values from -0.125 to 0.125
- up_weight: bfloat16 [32, 768, 2048], P('fsdp', 'tp'), may hold values from -0.125 to 0.125
- down_weight: bfloat16 [32, 768, 2048], P('fsdp', 'tp'), may hold values from -0.625 to 0.625
- cotangent: bfloat16 [8192, 2048], P(('fsdp', 'tp')), may hold values from -6 to 6
Outputs:
- output: bfloat16 [8192, 2048], P(('fsdp', 'tp'))
- input_grad: bfloat16 [8192, 2048], P(('fsdp', 'tp'))
- first_gain_grad: float32 [2048], P(('fsdp', 'tp'))
- query_weight_grad: float32 [2048, 4096], P('fsdp', 'tp')
- key_weight_grad: float32 [2048, 512], P('fsdp', 'tp')
- value_weight_grad: float32 [2048, 512], P('fsdp', 'tp')
- query_gain_grad: float32 [128], P(('fsdp', 'tp'))
- key_gain_grad: float32 [128], P(('fsdp', 'tp'))
- output_weight_grad: float32 [2048, 4096], P('fsdp', 'tp')
- second_gain_grad: float32 [2048], P(('fsdp', 'tp'))
- router_grad: float32 [2048, 32], P(('fsdp', 'tp'))
- gate_weight_grad: float32 [32, 768, 2048], P('fsdp', 'tp')
- up_weight_grad: float32 [32, 768, 2048], P('fsdp', 'tp')
- down_weight_grad: float32 [32, 768, 2048], P('fsdp', 'tp')
Inputs may be any that keep to these rules, and one draw needn't show every extreme that they name: Each row of expert_ids names 8 different experts. `segments`: segment numbers never fall along a sequence.
All inputs are finite; a program needn't handle non-finite values.
Results may differ from a plain program's by a relative error of at most 0.035.
Values may be sent and summed in bfloat16 or wider, within the bound.
No kernel may reach another device: no remote copies, remote signals or barrier semaphores. Data moves between devices by JAX's collectives and lax.ppermute only.
A program may use at most 576 MiB of HBM per device.

v0:
```python
import jax
import jax.numpy as jnp
from jax import lax
from jax.sharding import PartitionSpec as P

EPSILON = 1e-06
THETA = 1000000.0
NEG_BIG = -1e30


def rope_tables(segment_row, head_dim):
    length_total = segment_row.shape[0]
    token_index = jnp.arange(length_total, dtype=jnp.int32)
    change = jnp.concatenate(
        [jnp.ones((1,), jnp.int32), (segment_row[1:] != segment_row[:-1]).astype(jnp.int32)]
    )
    doc_start = lax.cummax(token_index * change, axis=0)
    position = (token_index - doc_start).astype(jnp.float32)
    half_dim = head_dim // 2
    inverse = THETA ** (-(jnp.arange(half_dim, dtype=jnp.float32) * 2.0) / head_dim)
    angles = position[:, None] * inverse[None, :]
    angles = jnp.concatenate([angles, angles], axis=1)
    return (jnp.cos(angles)[:, None, :], jnp.sin(angles)[:, None, :])


def rotate(values, cos_table, sin_table):
    half_dim = values.shape[-1] // 2
    turned = jnp.concatenate([-values[..., half_dim:], values[..., :half_dim]], axis=-1)
    return values * cos_table + turned * sin_table


def rotate_back(gradient, cos_table, sin_table):
    half_dim = gradient.shape[-1] // 2
    scaled = gradient * sin_table
    turned = jnp.concatenate([scaled[..., half_dim:], -scaled[..., :half_dim]], axis=-1)
    return gradient * cos_table + turned


def norm_forward(values):
    inverse = lax.rsqrt(jnp.mean(values * values, axis=-1, keepdims=True) + EPSILON)
    return (values * inverse, inverse)


def norm_back(gradient, scaled, inverse, gain_vec):
    weighted = gradient * gain_vec
    return inverse * (weighted - scaled * jnp.mean(weighted * scaled, axis=-1, keepdims=True))


def block_mask(segment_row, prefix_len, block_begin, block_row_span):
    length_total = segment_row.shape[0]
    query_pos = block_begin + jnp.arange(block_row_span, dtype=jnp.int32)
    key_pos = jnp.arange(length_total, dtype=jnp.int32)
    query_seg = lax.dynamic_slice_in_dim(segment_row, block_begin, block_row_span, 0)
    same_doc = query_seg[:, None] == segment_row[None, :]
    allowed = (key_pos[None, :] <= query_pos[:, None]) | (key_pos[None, :] < prefix_len)
    return same_doc & allowed


def block_scores(
    block_begin, query_head_rows, key_heads, segment_row, prefix_len, block_row_span, score_scale
):
    kv_count = key_heads.shape[1]
    head_dim = key_heads.shape[2]
    query_block_rows = lax.dynamic_slice_in_dim(
        query_head_rows, block_begin, block_row_span, 0
    ).reshape(block_row_span, kv_count, -1, head_dim)
    scores = (
        jnp.einsum(
            "bhgd,khd->hgbk", query_block_rows, key_heads, preferred_element_type=jnp.float32
        )
        * score_scale
    )
    visible = block_mask(segment_row, prefix_len, block_begin, block_row_span)
    return (query_block_rows, jnp.where(visible[None, None], scores, NEG_BIG))


def forward_block(
    block_begin,
    query_head_rows,
    key_heads,
    value_head_rows,
    segment_row,
    prefix_len,
    block_row_span,
    score_scale,
):
    query_block_rows, scores = block_scores(
        block_begin,
        query_head_rows,
        key_heads,
        segment_row,
        prefix_len,
        block_row_span,
        score_scale,
    )
    top_score = jnp.max(scores, axis=-1, keepdims=True)
    log_total = top_score + jnp.log(jnp.sum(jnp.exp(scores - top_score), axis=-1, keepdims=True))
    probs_low = jnp.exp(scores - log_total).astype(jnp.bfloat16)
    mixed_rows = jnp.einsum(
        "hgbk,khd->bhgd", probs_low, value_head_rows, preferred_element_type=jnp.float32
    )
    return (mixed_rows.reshape(block_row_span, -1), log_total[..., 0])


def backward_block(
    carried,
    inputs,
    query_head_rows,
    key_heads,
    value_head_rows,
    mixed_grad,
    segment_row,
    prefix_len,
    block_row_span,
    score_scale,
):
    key_acc, value_acc = carried
    block_begin, log_total = inputs
    kv_count = key_heads.shape[1]
    head_dim = key_heads.shape[2]
    query_block_rows, scores = block_scores(
        block_begin,
        query_head_rows,
        key_heads,
        segment_row,
        prefix_len,
        block_row_span,
        score_scale,
    )
    grad_block = lax.dynamic_slice_in_dim(mixed_grad, block_begin, block_row_span, 0).reshape(
        block_row_span, kv_count, -1, head_dim
    )
    probs = jnp.exp(scores - log_total[..., None])
    prob_grad = jnp.einsum(
        "bhgd,khd->hgbk", grad_block, value_head_rows, preferred_element_type=jnp.float32
    )
    score_grad = (probs * (prob_grad - jnp.sum(probs * prob_grad, axis=-1, keepdims=True))).astype(
        jnp.bfloat16
    )
    query_grad = (
        jnp.einsum("hgbk,khd->bhgd", score_grad, key_heads, preferred_element_type=jnp.float32)
        * score_scale
    )
    key_acc = (
        key_acc
        + jnp.einsum(
            "hgbk,bhgd->khd", score_grad, query_block_rows, preferred_element_type=jnp.float32
        )
        * score_scale
    )
    value_acc = value_acc + jnp.einsum(
        "hgbk,bhgd->khd", probs.astype(jnp.bfloat16), grad_block, preferred_element_type=jnp.float32
    )
    return ((key_acc, value_acc), query_grad.reshape(block_row_span, -1, head_dim))


def to_experts(buffer):
    return lax.all_to_all(buffer, "fsdp", split_axis=0, concat_axis=2, tiled=True)[0]


def collect_whole(values):
    returned = lax.all_to_all(values[None], "fsdp", split_axis=2, concat_axis=0, tiled=True)
    return returned.reshape(-1, values.shape[2])


def expert_forward(pieces):
    rows_in, gate_mat, up_mat, down_mat = pieces
    unit_count = gate_mat.shape[0]
    both_pre = jnp.einsum(
        "rd,fd->rf",
        rows_in,
        jnp.concatenate([gate_mat, up_mat], axis=0),
        preferred_element_type=jnp.float32,
    )
    gate_pre = both_pre[:, :unit_count]
    up_pre = both_pre[:, unit_count:]
    activated = (jax.nn.silu(gate_pre) * up_pre).astype(jnp.bfloat16)
    expert_part = jnp.dot(activated, down_mat, preferred_element_type=jnp.float32).astype(
        jnp.bfloat16
    )
    return (gate_pre, up_pre, activated, expert_part)


def expert_backward(pieces):
    rows_in, grad_in, gate_pre, up_pre, activated, gate_mat, up_mat, down_mat = pieces
    unit_count = gate_mat.shape[0]
    act_grad = jnp.einsum("rd,fd->rf", grad_in, down_mat, preferred_element_type=jnp.float32)
    down_grad = jnp.einsum("rf,rd->fd", activated, grad_in, preferred_element_type=jnp.float32)
    sigmoid_gate = jax.nn.sigmoid(gate_pre)
    gate_grad = (act_grad * up_pre * sigmoid_gate * (1.0 + gate_pre * (1.0 - sigmoid_gate))).astype(
        jnp.bfloat16
    )
    up_grad = (act_grad * gate_pre * sigmoid_gate).astype(jnp.bfloat16)
    both_grad = jnp.concatenate([gate_grad, up_grad], axis=1)
    both_wgrad = jnp.einsum("rf,rd->fd", both_grad, rows_in, preferred_element_type=jnp.float32)
    row_grad = jnp.einsum(
        "rf,fd->rd",
        both_grad,
        jnp.concatenate([gate_mat, up_mat], axis=0),
        preferred_element_type=jnp.float32,
    ).astype(jnp.bfloat16)
    return (row_grad, both_wgrad[:unit_count], both_wgrad[unit_count:], down_grad)


def local(
    tokens,
    segments,
    prefix,
    expert_ids,
    first_gain,
    query_weight,
    key_matrix,
    value_matrix,
    query_gain,
    key_gain,
    output_weight,
    second_gain,
    router,
    gate_weight,
    up_weight,
    down_weight,
    cotangent,
):
    tp_count = lax.axis_size("tp")
    fsdp_count = lax.axis_size("fsdp")
    tp_rank = lax.axis_index("tp")
    (
        first_all,
        query_all,
        key_all,
        value_all,
        qgain_all,
        kgain_all,
        output_all,
        second_all,
        router_all,
    ) = (
        lax.all_gather(first_gain, "fsdp", axis=0, tiled=True),
        lax.all_gather(query_weight, "fsdp", axis=0, tiled=True),
        lax.all_gather(key_matrix, "fsdp", axis=0, tiled=True),
        lax.all_gather(value_matrix, "fsdp", axis=0, tiled=True),
        lax.all_gather(query_gain, "fsdp", axis=0, tiled=True),
        lax.all_gather(key_gain, "fsdp", axis=0, tiled=True),
        lax.all_gather(output_weight, "fsdp", axis=0, tiled=True),
        lax.all_gather(second_gain, "fsdp", axis=0, tiled=True),
        lax.all_gather(router, "fsdp", axis=0, tiled=True),
    )
    gain_one = first_all.astype(jnp.float32)
    gain_two = second_all.astype(jnp.float32)
    gain_query = qgain_all.astype(jnp.float32)
    gain_key = kgain_all.astype(jnp.float32)
    own_rows = tokens.shape[0]
    row_start = tp_rank * own_rows
    seq_rows = lax.all_gather(tokens, "tp", axis=0, tiled=True)
    seq_len = seq_rows.shape[0]
    model_dim = seq_rows.shape[1]
    head_dim = gain_query.shape[0]
    query_count = query_all.shape[1] // head_dim
    kv_count = key_all.shape[1] // head_dim
    score_scale = head_dim ** (-0.5)
    block_row_span = min(512, seq_len)
    block_count = seq_len // block_row_span
    segment_row = segments[0]
    prefix_len = prefix[0]
    cos_table, sin_table = rope_tables(segment_row, head_dim)
    input_float = seq_rows.astype(jnp.float32)
    input_hat, input_inverse = norm_forward(input_float)
    first_normed = (input_hat * gain_one).astype(jnp.bfloat16)
    query_pre = jnp.dot(first_normed, query_all, preferred_element_type=jnp.float32).reshape(
        seq_len, query_count, head_dim
    )
    key_before_norm = jnp.dot(first_normed, key_all, preferred_element_type=jnp.float32).reshape(
        seq_len, kv_count, head_dim
    )
    value_head_rows = (
        jnp.dot(first_normed, value_all, preferred_element_type=jnp.float32)
        .astype(jnp.bfloat16)
        .reshape(seq_len, kv_count, head_dim)
    )
    query_hat, query_inverse = norm_forward(query_pre)
    key_hat, key_inverse = norm_forward(key_before_norm)
    query_head_rows = rotate(query_hat * gain_query, cos_table, sin_table).astype(jnp.bfloat16)
    key_heads = rotate(key_hat * gain_key, cos_table, sin_table).astype(jnp.bfloat16)
    starts = jnp.arange(block_count, dtype=jnp.int32) * block_row_span
    mixed_rows, log_totals = lax.map(
        lambda block_begin: forward_block(
            block_begin,
            query_head_rows,
            key_heads,
            value_head_rows,
            segment_row,
            prefix_len,
            block_row_span,
            score_scale,
        ),
        starts,
    )
    mixed_low = mixed_rows.reshape(seq_len, query_count * head_dim).astype(jnp.bfloat16)
    attended = lax.psum(
        jnp.einsum("sa,da->sd", mixed_low, output_all, preferred_element_type=jnp.float32).astype(
            jnp.bfloat16
        ),
        "tp",
    ).astype(jnp.float32)
    hidden = input_float + attended
    hidden_hat, hidden_inverse = norm_forward(hidden)
    normed_two = (hidden_hat * gain_two).astype(jnp.bfloat16)
    expert_total = router_all.shape[1]
    top_count = expert_ids.shape[1]
    capacity = (9 * top_count * seq_len + 8 * expert_total - 1) // (8 * expert_total)
    logits = jnp.dot(normed_two, router_all, preferred_element_type=jnp.float32)
    chosen_mask = expert_ids[:, :, None] == jnp.arange(expert_total, dtype=jnp.int32)[None, None, :]
    chosen = jnp.sum(jnp.where(chosen_mask, logits[:, None, :], 0.0), axis=-1)
    gate_probs = jax.nn.softmax(chosen, axis=-1)
    per_token = jnp.sum(chosen_mask.astype(jnp.int32), axis=1)
    earlier = jnp.cumsum(per_token, axis=0) - per_token
    slot_pos = jnp.sum(jnp.where(chosen_mask, earlier[:, None, :], 0), axis=-1)
    in_capacity = slot_pos < capacity
    empty_slot = expert_total * capacity
    slot_index = jnp.where(in_capacity, expert_ids * capacity + slot_pos, empty_slot)
    token_index = jnp.broadcast_to(jnp.arange(seq_len, dtype=jnp.int32)[:, None], expert_ids.shape)
    slot_token = (
        jnp.full((empty_slot,), seq_len, jnp.int32)
        .at[slot_index.reshape(-1)]
        .set(token_index.reshape(-1), mode="drop")
    )
    slot_gate = (
        jnp.zeros((empty_slot,), jnp.float32)
        .at[slot_index.reshape(-1)]
        .set(gate_probs.reshape(-1), mode="drop")
    )
    local_experts = gate_weight.shape[0]
    send_shape = (fsdp_count, local_experts, capacity, model_dim)
    zero_row = jnp.zeros((1, model_dim), jnp.bfloat16)
    zero_one = jnp.zeros((1,), jnp.float32)
    padded_two = jnp.concatenate([normed_two, zero_row], axis=0)
    rows_in = to_experts(padded_two[slot_token].reshape(send_shape))
    gate_pre, up_pre, activated, expert_part = lax.map(
        expert_forward, (rows_in, gate_weight, up_weight, down_weight)
    )
    returned = collect_whole(expert_part)
    expert_mix = jax.ops.segment_sum(
        returned.astype(jnp.float32) * slot_gate[:, None], slot_token, num_segments=seq_len + 1
    )[:seq_len]
    expert_own = lax.psum_scatter(
        expert_mix.astype(jnp.bfloat16), "tp", scatter_dimension=0, tiled=True
    ).astype(jnp.float32)
    hidden_own = lax.dynamic_slice_in_dim(hidden, row_start, own_rows, 0)
    output = (hidden_own + expert_own).astype(jnp.bfloat16)
    grad_rows = lax.all_gather(cotangent, "tp", axis=0, tiled=True)
    grad_float = grad_rows.astype(jnp.float32)
    grad_pad = jnp.concatenate([grad_rows, zero_row], axis=0)
    slot_rows = grad_pad[slot_token]
    slot_grad = (
        (slot_rows.astype(jnp.float32) * slot_gate[:, None])
        .astype(jnp.bfloat16)
        .reshape(send_shape)
    )
    grad_in = to_experts(slot_grad)
    row_grad, gate_wgrad, up_wgrad, down_wgrad = lax.map(
        expert_backward,
        (rows_in, grad_in, gate_pre, up_pre, activated, gate_weight, up_weight, down_weight),
    )
    back_rows = collect_whole(row_grad)
    expert_input_part = jax.ops.segment_sum(
        back_rows.astype(jnp.float32), slot_token, num_segments=seq_len + 1
    )[:seq_len]
    slot_dot = jnp.sum(slot_rows.astype(jnp.float32) * returned.astype(jnp.float32), axis=-1)
    prob_part = jnp.concatenate([slot_dot, zero_one], axis=0)[slot_index]
    expert_input_grad, prob_grad = (
        lax.psum(expert_input_part.astype(jnp.bfloat16), "tp").astype(jnp.float32),
        lax.psum(prob_part.astype(jnp.bfloat16), "tp").astype(jnp.float32),
    )
    chosen_grad = gate_probs * (prob_grad - jnp.sum(gate_probs * prob_grad, axis=-1, keepdims=True))
    logit_grad = jnp.sum(jnp.where(chosen_mask, chosen_grad[:, :, None], 0.0), axis=1).astype(
        jnp.bfloat16
    )
    normed_two_grad = expert_input_grad + jnp.einsum(
        "se,de->sd", logit_grad, router_all, preferred_element_type=jnp.float32
    )
    hidden_grad = grad_float + norm_back(normed_two_grad, hidden_hat, hidden_inverse, gain_two)
    second_part = jnp.sum(
        lax.dynamic_slice_in_dim(normed_two_grad * hidden_hat, row_start, own_rows, 0), axis=0
    )
    router_part = jnp.einsum(
        "sd,se->de",
        lax.dynamic_slice_in_dim(normed_two, row_start, own_rows, 0),
        lax.dynamic_slice_in_dim(logit_grad, row_start, own_rows, 0),
        preferred_element_type=jnp.float32,
    )
    attended_grad = hidden_grad.astype(jnp.bfloat16)
    output_wgrad = jnp.einsum(
        "sd,sa->da", attended_grad, mixed_low, preferred_element_type=jnp.float32
    )
    mixed_grad = jnp.dot(attended_grad, output_all, preferred_element_type=jnp.float32).astype(
        jnp.bfloat16
    )
    zero_heads = jnp.zeros((seq_len, kv_count, head_dim), jnp.float32)
    (key_turn_grad, value_grad), query_turn_grad = lax.scan(
        lambda carried, inputs: backward_block(
            carried,
            inputs,
            query_head_rows,
            key_heads,
            value_head_rows,
            mixed_grad,
            segment_row,
            prefix_len,
            block_row_span,
            score_scale,
        ),
        (zero_heads, zero_heads),
        (starts, log_totals),
    )
    query_turn_grad = query_turn_grad.reshape(seq_len, query_count, head_dim)
    query_norm_grad = rotate_back(query_turn_grad, cos_table, sin_table)
    key_norm_grad = rotate_back(key_turn_grad, cos_table, sin_table)
    query_gain_part = jnp.sum(query_norm_grad * query_hat, axis=(0, 1))
    key_gain_part = jnp.sum(key_norm_grad * key_hat, axis=(0, 1))
    query_pre_grad = (
        norm_back(query_norm_grad, query_hat, query_inverse, gain_query)
        .astype(jnp.bfloat16)
        .reshape(seq_len, -1)
    )
    key_pre_grad = (
        norm_back(key_norm_grad, key_hat, key_inverse, gain_key)
        .astype(jnp.bfloat16)
        .reshape(seq_len, -1)
    )
    value_low = value_grad.astype(jnp.bfloat16).reshape(seq_len, -1)
    query_wgrad = jnp.einsum(
        "sd,sa->da", first_normed, query_pre_grad, preferred_element_type=jnp.float32
    )
    key_wgrad = jnp.einsum(
        "sd,sa->da", first_normed, key_pre_grad, preferred_element_type=jnp.float32
    )
    value_wgrad = jnp.einsum(
        "sd,sa->da", first_normed, value_low, preferred_element_type=jnp.float32
    )
    normed_one_grad = (
        jnp.einsum("sa,da->sd", query_pre_grad, query_all, preferred_element_type=jnp.float32)
        + jnp.einsum("sa,da->sd", key_pre_grad, key_all, preferred_element_type=jnp.float32)
        + jnp.einsum("sa,da->sd", value_low, value_all, preferred_element_type=jnp.float32)
    )
    first_part = jnp.sum(normed_one_grad * input_hat, axis=0)
    input_part = norm_back(normed_one_grad, input_hat, input_inverse, gain_one)
    input_sum, first_sum, qgain_sum, kgain_sum, second_sum, router_sum = (
        lax.psum_scatter(
            input_part.astype(jnp.bfloat16), "tp", scatter_dimension=0, tiled=True
        ).astype(jnp.float32),
        lax.psum_scatter(
            first_part.reshape(fsdp_count, tp_count, -1).astype(jnp.bfloat16),
            "tp",
            scatter_dimension=1,
            tiled=True,
        ).astype(jnp.float32),
        lax.psum_scatter(
            query_gain_part.reshape(fsdp_count, tp_count, -1).astype(jnp.bfloat16),
            "tp",
            scatter_dimension=1,
            tiled=True,
        ).astype(jnp.float32),
        lax.psum_scatter(
            key_gain_part.reshape(fsdp_count, tp_count, -1).astype(jnp.bfloat16),
            "tp",
            scatter_dimension=1,
            tiled=True,
        ).astype(jnp.float32),
        lax.psum_scatter(
            second_part.reshape(fsdp_count, tp_count, -1).astype(jnp.bfloat16),
            "tp",
            scatter_dimension=1,
            tiled=True,
        ).astype(jnp.float32),
        lax.psum_scatter(
            router_part.reshape(fsdp_count, tp_count, -1, expert_total).astype(jnp.bfloat16),
            "tp",
            scatter_dimension=1,
            tiled=True,
        ).astype(jnp.float32),
    )
    input_grad = (lax.dynamic_slice_in_dim(hidden_grad, row_start, own_rows, 0) + input_sum).astype(
        jnp.bfloat16
    )
    (
        query_wshard,
        key_wshard,
        value_wshard,
        output_wshard,
        first_shard,
        qgain_shard,
        kgain_shard,
        second_shard,
        router_shard,
    ) = (
        lax.psum_scatter(
            query_wgrad.astype(jnp.bfloat16), "fsdp", scatter_dimension=0, tiled=True
        ).astype(jnp.float32),
        lax.psum_scatter(
            key_wgrad.astype(jnp.bfloat16), "fsdp", scatter_dimension=0, tiled=True
        ).astype(jnp.float32),
        lax.psum_scatter(
            value_wgrad.astype(jnp.bfloat16), "fsdp", scatter_dimension=0, tiled=True
        ).astype(jnp.float32),
        lax.psum_scatter(
            output_wgrad.astype(jnp.bfloat16), "fsdp", scatter_dimension=0, tiled=True
        ).astype(jnp.float32),
        lax.psum_scatter(
            first_sum.astype(jnp.bfloat16), "fsdp", scatter_dimension=0, tiled=True
        ).astype(jnp.float32),
        lax.psum_scatter(
            qgain_sum.astype(jnp.bfloat16), "fsdp", scatter_dimension=0, tiled=True
        ).astype(jnp.float32),
        lax.psum_scatter(
            kgain_sum.astype(jnp.bfloat16), "fsdp", scatter_dimension=0, tiled=True
        ).astype(jnp.float32),
        lax.psum_scatter(
            second_sum.astype(jnp.bfloat16), "fsdp", scatter_dimension=0, tiled=True
        ).astype(jnp.float32),
        lax.psum_scatter(
            router_sum.astype(jnp.bfloat16), "fsdp", scatter_dimension=0, tiled=True
        ).astype(jnp.float32),
    )
    return (
        output,
        input_grad,
        first_shard.reshape(-1),
        query_wshard,
        key_wshard,
        value_wshard,
        qgain_shard.reshape(-1),
        kgain_shard.reshape(-1),
        output_wshard,
        second_shard.reshape(-1),
        router_shard.reshape(-1, expert_total),
        gate_wgrad,
        up_wgrad,
        down_wgrad,
    )


def solution(mesh):
    placed = (
        P(("fsdp", "tp"), None),
        P("fsdp", None),
        P("fsdp"),
        P("fsdp", None),
        P("fsdp"),
        P("fsdp", "tp"),
        P("fsdp", "tp"),
        P("fsdp", "tp"),
        P("fsdp"),
        P("fsdp"),
        P("fsdp", "tp"),
        P("fsdp"),
        P("fsdp", None),
        P("fsdp", "tp", None),
        P("fsdp", "tp", None),
        P("fsdp", "tp", None),
        P(("fsdp", "tp"), None),
    )
    return jax.shard_map(
        local,
        mesh=mesh,
        in_specs=placed,
        out_specs=(
            P(("fsdp", "tp"), None),
            P(("fsdp", "tp"), None),
            P(("fsdp", "tp")),
            P("fsdp", "tp"),
            P("fsdp", "tp"),
            P("fsdp", "tp"),
            P(("fsdp", "tp")),
            P(("fsdp", "tp")),
            P("fsdp", "tp"),
            P(("fsdp", "tp")),
            P(("fsdp", "tp"), None),
            P("fsdp", "tp", None),
            P("fsdp", "tp", None),
            P("fsdp", "tp", None),
        ),
        check_vma=False,
    )
```

profile of v0, /device:TPU:0, one launch (start us, length us, event | category | flops | bytes accessed | tf_op | source)
XLA Modules:
  0.0 3628.5 jit_solution(4315419427038029357)
XLA Ops:
  155.6 43.4 %while.59 = (s32[]{:T(128)}, bf16[2,512,1024]{2,1,0:T(8,128)(2,1)}, f32[2,1,8,512]{3,2,1,0:T(8,128)S(1)}, s32[2]{0:T(128)S(1)}, s32[1024]{0:T(1024)S(1)}, /*inde...) while((s32[]{:T(128)}, bf16[2,512,1024]{2,1,0:T(8,128)(2,1)}, ...), condition=%wide.region_8.9_spmd, body=%wide.region_5.0_spmd.sunk | while | flops 2195715584 | bytes 59392700 | solution.py:285
  261.5 103.0 %all-reduce.20.cloned.1.call-done = bf16[1024,2048]{1,0:T(8,128)(2,1)} async-done(((bf16[1024,2048]{1,0:T(8,128)(2,1)}), bf16[1024,2048]{1,0:T(8,128)(2,1)}) %all-reduce.20.cloned.1.call-update) | async-done | bytes 4194320 | tf_op jit(solution)/shard_map/psum | solution.py:299
  382.8 71.6 %gather_fusion = bf16[9216,2048]{1,0:T(8,128)(2,1)} fusion(bf16[1025,2048]{1,0:T(8,128)(2,1)} %concatenate.84, s32[9216]{0:T(1024)S(1)} %fusion.148), kind=kCustom, calls=%fused_computation | custom fusion | bytes 75534336 | tf_op jit(solution)/shard_map/gather | solution.py:337
  462.2 408.6 %all-to-all-done = bf16[8,4,288,2048]{3,2,1,0:T(8,128)(2,1)} async-done(((bf16[8,4,288,2048]{3,2,1,0:T(8,128)(2,1)}), bf16[8,4,288,2048]{3,2,1,0:T(8,128)(2,1)}, u32[]{:S(2)}, u32[]{:S(2)}) %all-to-all-start) | async-done | bytes 37748768 | tf_op jit(solution)/shard_map/all_to_all | solution.py:158
  908.6 72.6 %while.60 = (s32[]{:T(128)}, f32[4,2304,192]{1,2,0:T(8,128)}, f32[4,2304,192]{1,2,0:T(8,128)}, bf16[4,2304,192]{1,2,0:T(8,128)(2,1)}, bf16[4,2304,2048]{2,1,0:T(...) while((s32[]{:T(128)}, f32[4,2304,192]{1,2,0:T(8,128)}, ...), condition=%wide.region_17.18_spmd, body=%wide.region_16.17_spmd.sunk | while | flops 5446336512 | bytes 41192040 | solution.py:338
  981.3 47.1 %copy.259 = bf16[4,2304,2048]{2,0,1:T(4,128)(2,1)} copy(bf16[4,2304,2048]{2,1,0:T(8,128)(2,1)} %get-tuple-element.257) | data formatting | bytes 75497472 | tf_op jit(solution)/shard_map/while | solution.py:338
  1037.0 411.1 %all_gather.42 = bf16[2048,32]{0,1:T(8,128)(2,1)S(1)} all-gather(bf16[256,32]{0,1:T(8,128)(2,1)S(1)} %copy-done.64), channel_id=1, replica_groups=mesh['fsdp'=8,'tp'=4] {'fsdp'}, dimensions={0}, use_global_device_ids=true | all-gather | bytes 147456 | tf_op jit(solution)/shard_map/all_gather | solution.py:246
  1453.5 72.0 %gather_fusion.1 = bf16[9216,2048]{1,0:T(8,128)(2,1)} fusion(bf16[1025,2048]{1,0:T(8,128)(2,1)} %concatenate.85, s32[9216]{0:T(1024)S(1)} %copy-done.40), kind=kCustom, calls=%fused_computation.1 | custom fusion | bytes 75534336 | tf_op jit(solution)/shard_map/gather | solution.py:353
  1525.5 36.6 %convert_element_type.324 = f32[9216,2048]{1,0:T(8,128)} convert(bf16[9216,2048]{1,0:T(8,128)(2,1)} %gather_fusion.1) | non-fusion elementwise | flops 18874368 | bytes 113246208 | tf_op jit(solution)/shard_map/convert_element_type | solution.py:355
  1601.9 63.6 %fusion.95 = bf16[8,4,288]{2,1,0:T(4,128)(2,1)S(1)} fusion(f32[8,1,4,288,2048]{4,3,2,0,1:T(8,128)} %bitcast.69, f32[1,4,8,288,2048]{4,1,3,2,0:T(4,128)} %convert.27), kind=kLoop, calls=%fused_computation.131 | loop fusion | flops 37739520 | bytes 151013376 | tf_op jit(solution)/shard_map/reduce_sum | solution.py:368
  1665.6 50.7 %gather_fusion.2 = bf16[8192]{0:T(1024)(128)(2,1)S(1)} fusion(bf16[9217]{0:T(1024)(128)(2,1)S(1)} %pad_maximum_fusion.6, s32[8192]{0:T(1024)S(1)} %copy-done.20), kind=kCustom, calls=%fused_computation.2 | custom fusion | bytes 65536 | tf_op jit(solution)/shard_map/gather | solution.py:369
  1765.0 36.3 %multiply_convert_fusion.1 = bf16[8,4,288,2048]{3,2,1,0:T(8,128)(2,1)} fusion(f32[8,4,288,2048]{3,2,1,0:T(8,128)} %bitcast.61, f32[8,4,288]{2,1,0:T(4,128)S(1)} %mul.479), kind=kLoop, calls=%fused_computation.132 | loop fusion | flops 37748736 | bytes 113283072 | tf_op jit(solution)/shard_map/convert_element_type | solution.py:356
  1809.1 408.6 %all-to-all-done.2 = bf16[8,4,288,2048]{3,2,1,0:T(8,128)(2,1)} async-done(((bf16[8,4,288,2048]{3,2,1,0:T(8,128)(2,1)}), bf16[8,4,288,2048]{3,2,1,0:T(8,128)(2,1)}, u32[]{:S(2)}, u32[]{:S(2)}) %all-to-all-start.2) | async-done | bytes 37748768 | tf_op jit(solution)/shard_map/all_to_all | solution.py:158
  2255.3 132.8 %while.61 = (s32[]{:T(128)}, bf16[4,2304,2048]{2,1,0:T(8,128)(2,1)}, f32[4,192,2048]{2,1,0:T(8,128)}, f32[4,192,2048]{2,1,0:T(8,128)}, f32[4,192,2048]{2,1,0:T(8...) while((s32[]{:T(128)}, ...), condition=%wide.region_25.26_spmd, body=%wide.region_24.25_spmd.sunk | while | flops 10892328960 | bytes 64000648 | solution.py:360
  2388.1 47.1 %copy.258 = bf16[4,2304,2048]{2,0,1:T(4,128)(2,1)} copy(bf16[4,2304,2048]{2,1,0:T(8,128)(2,1)} %get-tuple-element.261) | data formatting | bytes 75497472 | tf_op jit(solution)/shard_map/while | solution.py:360
  2443.6 39.3 %copy.190 = f32[1,4,8,288,2048]{4,3,1,2,0:T(8,128)} copy(bf16[1,4,8,288,2048]{4,1,3,2,0:T(4,128)(2,1)} %bitcast.129) | data formatting | bytes 113246208 | tf_op jit(solution)/shard_map/convert_element_type | solution.py:343
  2485.6 365.8 %all-to-all-done.3 = bf16[1,4,2304,2048]{3,1,0,2:T(4,128)(2,1)} async-done(((bf16[1,4,2304,2048]{3,1,0,2:T(4,128)(2,1)}), bf16[1,4,2304,2048]{3,1,0,2:T(4,128)(2,1)}, u32[]{:S(2)}, u32[]{:S(2)}) %all-to-all-start.3) | async-done | bytes 37748768 | tf_op jit(solution)/shard_map/all_to_all | solution.py:162
  2851.4 39.1 %copy.195 = f32[1,4,8,288,2048]{4,3,1,2,0:T(8,128)} copy(bf16[1,4,8,288,2048]{4,1,3,2,0:T(4,128)(2,1)} %bitcast.132) | data formatting | bytes 113246208 | tf_op jit(solution)/shard_map/convert_element_type | solution.py:366
  2890.5 118.5 %scatter_custom_fusion.3 = f32[1025,2048]{1,0:T(8,128)} fusion(s32[9216]{0:T(1024)} %copy-done.49, f32[9216,2048]{1,0:T(8,128)} %bitcast.68, f32[]{:T(128)} %constant.92.clone.1), kind=kCustom, calls=%fused_computation.159 | custom fusion | flops 18874368 | bytes 8397312 | tf_op jit(solution)/shard_map/scatter-add | solution.py:365
  3015.8 49.6 %bitcast_multiply_fusion.4 = f32[9216,2048]{1,0:T(8,128)} fusion(f32[1,4,8,288,2048]{4,3,1,2,0:T(8,128)} %copy.190, f32[9216]{0:T(1024)S(1)} %copy-done.42), kind=kLoop, calls=%fused_computation.129 | loop fusion | flops 18874368 | bytes 151031808 | tf_op jit(solution)/shard_map/mul | solution.py:343
  3065.4 118.1 %scatter_custom_fusion.2 = f32[1025,2048]{1,0:T(8,128)} fusion(s32[9216]{0:T(1024)} %copy-done.49, f32[9216,2048]{1,0:T(8,128)} %bitcast_multiply_fusion.4, f32[]{:T(128)} %constant.92.clone.1), kind=kCustom, calls=%fused_computation.161 | custom fusion | flops 18874368 | bytes 8397312 | tf_op jit(solution)/shard_map/scatter-add | solution.py:342
  3217.2 100.1 %while.62 = (s32[]{:T(128)}, f32[1024,1,128]{0,2,1:T(8,128)}, f32[1024,1,128]{0,2,1:T(8,128)}, f32[2,512,8,128]{3,1,2,0:T(8,128)}, s32[2]{0:T(128)S(1)}, /*index...) while((s32[]{:T(128)}, f32[1024,1,128]{0,2,1:T(8,128)}, ...), condition=%wide.region_35.36_spmd.clone, body=%wide.region_33.35_spmd.clone.sunk | while | flops 5409732096 | bytes 183468944 | solution.py:399
  3499.0 40.5 %reduce-scatter.13.cloned.1.call-done = bf16[256,1024]{1,0:T(8,128)(2,1)} async-done(((bf16[2048,1024]{1,0:T(8,128)(2,1)}), bf16[256,1024]{1,0:T(8,128)(2,1)}) %reduce-scatter.13.cloned.1.call-update) | async-done | bytes 524304 | tf_op jit(solution)/shard_map/reduce_scatter | solution.py:496
  3541.6 77.0 %reduce-scatter.11.cloned.1.call-done = bf16[256,2048]{1,0:T(8,128)(2,1)} async-done(((bf16[1024,2048]{1,0:T(8,128)(2,1)}), bf16[256,2048]{1,0:T(8,128)(2,1)}) %reduce-scatter.11.cloned.1.call-update) | async-done | bytes 1048592 | tf_op jit(solution)/shard_map/reduce_scatter | solution.py:448
  (491 shorter events, 999.9 us)
Async XLA Ops:
  7.2 85.9 %all-gather.7.cloned.1.call-start = ((), (), s32[]{:S(2)}) async-start(), calls=%async_computation.11 | async-start | bytes 5242880 | tf_op jit(solution)/shard_map/all_gather | solution.py:254
  7.9 122.1 %all-gather.9.cloned.1.call-start = ((), (), s32[]{:S(2)}) async-start(), calls=%async_computation.12 | async-start | bytes 4718592 | tf_op jit(solution)/shard_map/all_gather | solution.py:239
  8.7 190.3 %all-gather.11.cloned.1.call-start = ((), (), s32[]{:S(2)}) async-start(), calls=%async_computation.13 | async-start | bytes 4718592 | tf_op jit(solution)/shard_map/all_gather | solution.py:244
  9.4 355.1 %all-reduce.20.cloned.1.call-start = ((), (), s32[]{:S(2)}) async-start(), calls=%async_computation.14 | async-start | bytes 8388608 | tf_op jit(solution)/shard_map/psum | solution.py:299
  49.7 101.7 %copy-start.66 = (f32[128]{0:T(128)}, f32[128]{0:T(128)S(1)}, u32[]{:S(2)}) copy-start(f32[128]{0:T(128)S(1)} %convert_element_type.260) | copy-start | bytes 1540
  218.9 150.7 %copy-start.54 = (f32[8,1,256]{2,1,0:T(1,128)}, f32[8,1,256]{2,1,0:T(1,128)S(1)}, u32[]{:S(2)}) copy-start(f32[8,1,256]{2,1,0:T(1,128)S(1)} %convert_element_type.335) | copy-start | bytes 24580
  261.5 108.1 %copy-start.49 = (s32[9216]{0:T(1024)}, s32[9216]{0:T(1024)S(1)}, u32[]{:S(2)}) copy-start(s32[9216]{0:T(1024)S(1)} %scatter_custom_fusion) | copy-start | bytes 110596
  261.5 121.3 %copy-start.39 = (s32[9216]{0:T(1024)}, s32[9216]{0:T(1024)S(1)}, u32[]{:S(2)}) copy-start(s32[9216]{0:T(1024)S(1)} %fusion.148) | copy-start | bytes 110596
  454.4 416.4 %all-to-all-start = ((bf16[8,4,288,2048]{3,2,1,0:T(8,128)(2,1)}), bf16[8,4,288,2048]{3,2,1,0:T(8,128)(2,1)}, u32[]{:S(2)}, u32[]{:S(2)}) async-start(bf16[8,4,288,2048]{3,2,1,0:T(8,128)(2,1)} %bitcast.517), calls=%async_computation | async-start | bytes 75497472 | tf_op jit(solution)/shard_map/all_to_all | solution.py:158
  1028.3 537.6 %all-to-all-start.1 = ((bf16[1,4,2304,2048]{3,1,0,2:T(4,128)(2,1)}), bf16[1,4,2304,2048]{3,1,0,2:T(4,128)(2,1)}, u32[]{:S(2)}, u32[]{:S(2)}) async-start(bf16[1,4,2304,2048]{3,1,0,2:T(4,128)(2,1)} %bitcast.519), calls=%async_computation.1 | async-start | bytes 75497472 | tf_op jit(solution)/shard_map/all_to_all | solution.py:162
  1035.9 412.8 %all-gather.13.cloned.1.call-start = ((), (), s32[]{:S(2)}) async-start(), calls=%async_computation.16 | async-start | bytes 5242880 | tf_op jit(solution)/shard_map/all_gather | solution.py:350
  1448.0 114.1 %copy-start.32 = (bf16[2048,32]{0,1:T(8,128)(2,1)}, bf16[2048,32]{0,1:T(8,128)(2,1)S(1)}, u32[]{:S(2)}) copy-start(bf16[2048,32]{0,1:T(8,128)(2,1)S(1)} %all_gather.42) | copy-start | bytes 393220
  1801.4 416.3 %all-to-all-start.2 = ((bf16[8,4,288,2048]{3,2,1,0:T(8,128)(2,1)}), bf16[8,4,288,2048]{3,2,1,0:T(8,128)(2,1)}, u32[]{:S(2)}, u32[]{:S(2)}) async-start(bf16[8,4,288,2048]{3,2,1,0:T(8,128)(2,1)} %multiply_convert_fusion.1), calls=%async_computation.3 | async-start | bytes 75497472 | tf_op jit(solution)/shard_map/all_to_all | solution.py:158
  2435.2 416.2 %all-to-all-start.3 = ((bf16[1,4,2304,2048]{3,1,0,2:T(4,128)(2,1)}), bf16[1,4,2304,2048]{3,1,0,2:T(4,128)(2,1)}, u32[]{:S(2)}, u32[]{:S(2)}) async-start(bf16[1,4,2304,2048]{3,1,0,2:T(4,128)(2,1)} %bitcast.518), calls=%async_computation.4 | async-start | bytes 75497472 | tf_op jit(solution)/shard_map/all_to_all | solution.py:162
  2442.8 746.9 %all-reduce.22.cloned.1.call-start = ((), (), s32[]{:S(2)}) async-start(), calls=%async_computation.23 | async-start | bytes 8912896 | tf_op jit(solution)/shard_map/psum | solution.py:371
  3015.0 425.6 %reduce-scatter.9.cloned.1.call-start = ((), (), s32[]{:S(2)}) async-start(), calls=%async_computation.15 | async-start | bytes 5242880 | tf_op jit(solution)/shard_map/reduce_scatter | solution.py:345
  3189.5 303.0 %reduce-scatter.21.cloned.1.call-start = ((), (), s32[]{:S(2)}) async-start(), calls=%async_computation.22 | async-start | bytes 73728 | tf_op jit(solution)/shard_map/reduce_scatter | solution.py:520
  3217.1 103.2 %copy-start.48 = (f32[1024]{0:T(1024)S(1)}, f32[1024]{0:T(1024)}, u32[]{:S(2)}) copy-start(f32[1024]{0:T(1024)} %copy-done.47) | copy-start | bytes 12292
  3217.1 103.2 %copy-start.69 = (f32[128]{0:T(128)S(1)}, f32[128]{0:T(128)}, u32[]{:S(2)}) copy-start(f32[128]{0:T(128)} %copy-done.68) | copy-start | bytes 1540
  3323.6 170.2 %reduce-scatter.15.cloned.1.call-start = ((), (), s32[]{:S(2)}) async-start(), calls=%async_computation.19 | async-start | bytes 589824 | tf_op jit(solution)/shard_map/reduce_scatter | solution.py:499
  3328.0 167.3 %reduce-scatter.17.cloned.1.call-start = ((), (), s32[]{:S(2)}) async-start(), calls=%async_computation.20 | async-start | bytes 589824 | tf_op jit(solution)/shard_map/reduce_scatter | solution.py:502
  3332.6 164.1 %reduce-scatter.19.cloned.1.call-start = ((), (), s32[]{:S(2)}) async-start(), calls=%async_computation.21 | async-start | bytes 4718592 | tf_op jit(solution)/shard_map/reduce_scatter | solution.py:505
  3342.3 197.1 %reduce-scatter.13.cloned.1.call-start = ((), (), s32[]{:S(2)}) async-start(), calls=%async_computation.18 | async-start | bytes 4718592 | tf_op jit(solution)/shard_map/reduce_scatter | solution.py:496
  3420.7 197.9 %reduce-scatter.11.cloned.1.call-start = ((), (), s32[]{:S(2)}) async-start(), calls=%async_computation.17 | async-start | bytes 5242880 | tf_op jit(solution)/shard_map/reduce_scatter | solution.py:448
  (80 other events, 1093.6 us)
Sparse Core Ops, SparseCore 0:
  9.6 83.4 all-gather.6
  94.9 35.0 all-gather.8
  131.9 36.5 all-gather.10
  209.4 155.0 all-reduce.19
  1038.0 80.1 all-gather.12
  3015.2 159.8 all-reduce.21
  3189.6 74.7 reduce-scatter.8
  3323.7 31.4 reduce-scatter.20
  3358.9 34.1 reduce-scatter.14
  3396.0 34.1 reduce-scatter.16
  3433.6 51.3 reduce-scatter.18
  3488.2 51.2 reduce-scatter.12
  3541.7 76.7 reduce-scatter.10
where the time goes:
time: 3640 us; the launch traced here: 3630 us
  waiting for transfers between devices  1460 us (40%)
  local copies, waits for them, and re-layouts  642 us (18%)
  other arithmetic  610 us (17%)
  blocking collectives  519 us (14%)
  matrix products  340 us (9%)
    all_to_all x2, waiting for transfers between devices, to_experts(): lax.all_to_all(buffer, 'fsdp', split_axis=0, concat_axis=2, tiled=True)[0]  817 us
    all_gather x1, blocking collectives, local(): lax.all_gather(router, 'fsdp', axis=0, tiled=True)  411 us
    all_to_all x2, waiting for transfers between devices, collect_whole(): lax.all_to_all(values[None], 'fsdp', split_axis=2, concat_axis=0, tiled=T...  366 us
    scatter-add x1, other arithmetic, local(): jax.ops.segment_sum(back_rows.astype(jnp.float32), slot_token, num_segmen...  118 us
    scatter-add x1, other arithmetic, local(): jax.ops.segment_sum(returned.astype(jnp.float32) * slot_gate[:, None], sl...  118 us
    psum x1, waiting for transfers between devices, local(): lax.psum(jnp.einsum('sa,da->sd', mixed_low, output_all, preferred_element...  103 us
    reduce_scatter x1, waiting for transfers between devices, local(): lax.psum_scatter(input_part.astype(jnp.bfloat16), 'tp', scatter_dimension...  77 us
  transfers between devices with their start and end apart: 17, of which 8 were waited for; matrix products, arithmetic and copies ran while one was open for 20% of the time, Pallas kernels for 0%

commit v1 on v0

--- a/solution.py
+++ b/solution.py
@@ -1,6 +1,10 @@
+import functools
+
 import jax
 import jax.numpy as jnp
 from jax import lax
+from jax.experimental import pallas as pl
+from jax.experimental.pallas import tpu as pltpu
 from jax.sharding import PartitionSpec as P
 
 EPSILON = 1e-06
@@ -46,10 +50,9 @@
     return inverse * (weighted - scaled * jnp.mean(weighted * scaled, axis=-1, keepdims=True))
 
 
-def block_mask(segment_row, prefix_len, block_begin, block_row_span):
-    length_total = segment_row.shape[0]
-    query_pos = block_begin + jnp.arange(block_row_span, dtype=jnp.int32)
-    key_pos = jnp.arange(length_total, dtype=jnp.int32)
+def block_mask(segment_row, token_pos, prefix_len, block_begin, block_row_span):
+    query_pos = lax.dynamic_slice_in_dim(token_pos, block_begin, block_row_span, 0)
+    key_pos = token_pos
     query_seg = lax.dynamic_slice_in_dim(segment_row, block_begin, block_row_span, 0)
     same_doc = query_seg[:, None] == segment_row[None, :]
     allowed = (key_pos[None, :] <= query_pos[:, None]) | (key_pos[None, :] < prefix_len)
@@ -57,7 +60,14 @@
 
 
 def block_scores(
-    block_begin, query_head_rows, key_heads, segment_row, prefix_len, block_row_span, score_scale
+    block_begin,
+    query_head_rows,
+    key_heads,
+    segment_row,
+    token_pos,
+    prefix_len,
+    block_row_span,
+    score_scale,
 ):
     kv_count = key_heads.shape[1]
     head_dim = key_heads.shape[2]
@@ -70,7 +80,7 @@
         )
         * score_scale
     )
-    visible = block_mask(segment_row, prefix_len, block_begin, block_row_span)
+    visible = block_mask(segment_row, token_pos, prefix_len, block_begin, block_row_span)
     return (query_block_rows, jnp.where(visible[None, None], scores, NEG_BIG))
 
 
@@ -80,6 +90,7 @@
     key_heads,
     value_head_rows,
     segment_row,
+    token_pos,
     prefix_len,
     block_row_span,
     score_scale,
@@ -89,6 +100,7 @@
         query_head_rows,
         key_heads,
         segment_row,
+        token_pos,
         prefix_len,
         block_row_span,
         score_scale,
@@ -110,6 +122,7 @@
     value_head_rows,
     mixed_grad,
     segment_row,
+    token_pos,
     prefix_len,
     block_row_span,
     score_scale,
@@ -123,6 +136,7 @@
         query_head_rows,
         key_heads,
         segment_row,
+        token_pos,
         prefix_len,
         block_row_span,
         score_scale,
@@ -202,7 +216,7 @@
     return (row_grad, both_wgrad[:unit_count], both_wgrad[unit_count:], down_grad)
 
 
-def local(
+def exchanged(
     tokens,
     segments,
     prefix,
@@ -262,6 +276,7 @@
     block_count = seq_len // block_row_span
     segment_row = segments[0]
     prefix_len = prefix[0]
+    token_pos = jnp.arange(seq_len, dtype=jnp.int32)
     cos_table, sin_table = rope_tables(segment_row, head_dim)
     input_float = seq_rows.astype(jnp.float32)
     input_hat, input_inverse = norm_forward(input_float)
@@ -289,6 +304,7 @@
             key_heads,
             value_head_rows,
             segment_row,
+            token_pos,
             prefix_len,
             block_row_span,
             score_scale,
@@ -405,6 +421,7 @@
             value_head_rows,
             mixed_grad,
             segment_row,
+            token_pos,
             prefix_len,
             block_row_span,
             score_scale,
@@ -533,6 +550,475 @@
         output_wshard,
         second_shard.reshape(-1),
         router_shard.reshape(-1, expert_total),
+        gate_wgrad,
+        up_wgrad,
+        down_wgrad,
+    )
+
+
+def partners(count, mask):
+    return [(i, i ^ mask) for i in range(count)]
+
+
+def swap(values, axis, mask):
+    return lax.ppermute(values, axis, partners(lax.axis_size(axis), mask))
+
+
+def xor_order(values, index, axis):
+    count = values.shape[axis]
+    bit = 1
+    while bit < count:
+        shape = values.shape
+        split = values.reshape(shape[:axis] + (count // (2 * bit), 2, bit) + shape[axis + 1 :])
+        flipped = jnp.flip(split, axis + 1).reshape(shape)
+        values = jnp.where((index & bit) != 0, flipped, values)
+        bit *= 2
+    return values
+
+
+def plane_gather(block, odd):
+    side = swap(block, "fsdp", 2)
+    above = swap(block, "fsdp", 4)
+    corner = swap(side, "fsdp", 4) if odd else swap(above, "fsdp", 2)
+    gathered = []
+    for held in (block, side, above, corner):
+        gathered += [held, swap(held, "fsdp", 1)]
+    return gathered
+
+
+def add_low(*terms):
+    total = terms[0].astype(jnp.float32)
+    for term in terms[1:]:
+        total = total + term.astype(jnp.float32)
+    return total
+
+
+def plane_reduce(parts, odd):
+    low = jnp.bfloat16
+    own, side, above, corner = [
+        add_low(parts[m], swap(parts[m + 1], "fsdp", 1)).astype(low) for m in (0, 2, 4, 6)
+    ]
+    if odd:
+        side = add_low(side, swap(corner, "fsdp", 4)).astype(low)
+    else:
+        above = add_low(above, swap(corner, "fsdp", 2)).astype(low)
+    return add_low(own, swap(side, "fsdp", 2), swap(above, "fsdp", 4)).astype(low)
+
+
+def tp_gather(block):
+    return [block] + [swap(block, "tp", r) for r in range(1, lax.axis_size("tp"))]
+
+
+def tp_reduce(parts):
+    return add_low(parts[0], *[swap(parts[r], "tp", r) for r in range(1, len(parts))])
+
+
+def small_reduce(parts):
+    parts = parts[0::2] + swap(parts[1::2], "fsdp", 1)
+    parts = parts[0::2] + swap(parts[1::2], "fsdp", 2)
+    parts = parts[0] + swap(parts[1], "fsdp", 4)
+    parts = parts[0::2] + swap(parts[1::2], "tp", 1)
+    return parts[0] + swap(parts[1], "tp", 2)
+
+
+def turned_tables(position, head_dim):
+    half_dim = head_dim // 2
+    inverse = THETA ** (-(jnp.arange(half_dim, dtype=jnp.float32) * 2.0) / head_dim)
+    angles = position.astype(jnp.float32)[:, None] * inverse[None, :]
+    angles = jnp.concatenate([angles, angles], axis=1)
+    return (jnp.cos(angles)[:, None, :], jnp.sin(angles)[:, None, :])
+
+
+def dot_nn(a, b):
+    return lax.dot_general(a, b, (((1,), (0,)), ((), ())), preferred_element_type=jnp.float32)
+
+def dot_nt(a, b):
+    return lax.dot_general(a, b, (((1,), (1,)), ((), ())), preferred_element_type=jnp.float32)
+
+def expert_kernel(pair_count, local_experts, lane_pad, *refs):
+    count = 2 * pair_count
+    x_refs, refs = refs[:count], refs[count:]
+    c_refs, refs = refs[:count], refs[count:]
+    code_ref, router_ref, gate_ref, up_ref, down_ref = refs[:5]
+    refs = refs[5:]
+    row_refs, refs = refs[:count], refs[count:]
+    out_refs, refs = refs[:count], refs[count:]
+    mixed_ref, act_ref, xb, cb, rb, ob, prod, in_sem, out_sem = refs
+    rows = x_refs[0].shape[0]
+    span = 2 * rows
+    hidden, width = gate_ref.shape
+    per_expert = hidden // local_experts
+    step = pl.program_id(0)
+    slot = lax.rem(step, 2)
+
+    def loads(index, at):
+        for k in range(2):
+            where = pl.ds(k * rows, rows)
+            yield pltpu.make_async_copy(x_refs[index + k], xb.at[at, where], in_sem.at[at, 2 * k])
+            yield pltpu.make_async_copy(c_refs[index + k], cb.at[at, where], in_sem.at[at, 2 * k + 1])
+
+    def stores(index, at):
+        for k in range(2):
+            where = pl.ds(k * rows, rows)
+            yield pltpu.make_async_copy(rb.at[at, where], row_refs[index + k], out_sem.at[at, 2 * k])
+            yield pltpu.make_async_copy(ob.at[at, where], out_refs[index + k], out_sem.at[at, 2 * k + 1])
+
+    def start_loads(which, at):
+        for j in range(pair_count):
+            @pl.when(which == j)
+            def _(j=j):
+                for copy in loads(2 * j, at):
+                    copy.start()
+
+    @pl.when(step == 0)
+    def _():
+        start_loads(step, 0)
+
+    @pl.when(step + 1 < pair_count)
+    def _():
+        start_loads(step + 1, 1 - slot)
+
+    for copy in loads(0, slot):
+        copy.wait()
+
+    logits = dot_nn(xb[slot], router_ref[...])
+    code = code_ref[0].astype(jnp.float32)
+    chosen = code > 0.5
+    top = jnp.max(jnp.where(chosen, logits, -1e30), axis=1, keepdims=True)
+    powers = jnp.where(chosen, jnp.exp(logits - top), 0.0)
+    probs = powers / jnp.sum(powers, axis=1, keepdims=True)
+    kept = jnp.where(code > 1.5, probs, 0.0)
+    tile = min(256, hidden)
+
+    def hidden_step(j, carry):
+        at = pl.multiple_of(j * tile, tile)
+        cols = pl.ds(at, tile)
+        gate = dot_nt(xb[slot], gate_ref[cols, :])
+        up = dot_nt(xb[slot], up_ref[cols, :])
+        act_grad = dot_nt(cb[slot], down_ref[cols, :])
+        column = at + lax.broadcasted_iota(jnp.int32, (1, tile), 1)
+        weight = kept[:, 0:1]
+        for e in range(1, local_experts):
+            weight = jnp.where(column < e * per_expert, weight, kept[:, e : e + 1])
+        sigmoid = 1.0 / (1.0 + jnp.exp(-gate))
+        silu = gate * sigmoid
+        act = silu * up
+        act_grad = act_grad * weight
+        act_ref[:, cols] = (act * weight).astype(jnp.bfloat16)
+        prod[:, cols] = (act * act_grad).astype(jnp.bfloat16)
+        mixed_ref[:, cols] = (act_grad * up * (sigmoid + silu * (1.0 - sigmoid))).astype(jnp.bfloat16)
+        mixed_ref[:, pl.ds(pl.multiple_of(hidden + at, 128), tile)] = (act_grad * silu).astype(jnp.bfloat16)
+        return carry
+
+    lax.fori_loop(0, hidden // tile, hidden_step, 0)
+    owner = lax.broadcasted_iota(jnp.int32, (hidden, lane_pad), 0)
+    lane = lax.broadcasted_iota(jnp.int32, (hidden, lane_pad), 1) * per_expert
+    member = jnp.where((owner >= lane) & (owner < lane + per_expert), 1.0, 0.0).astype(jnp.bfloat16)
+    weighted = dot_nn(prod[...], member)
+    total = jnp.sum(weighted, axis=1, keepdims=True)
+    mixed_ref[:, 2 * hidden :] = (weighted - probs * total).astype(jnp.bfloat16)
+
+    @pl.when(step >= 2)
+    def _():
+        for copy in stores(0, slot):
+            copy.wait()
+
+    out_tile = min(256, width)
+
+    def width_step(j, carry):
+        cols = pl.ds(pl.multiple_of(j * out_tile, out_tile), out_tile)
+        row_grad = dot_nn(mixed_ref[:, :hidden], gate_ref[:, cols])
+        row_grad = row_grad + dot_nn(mixed_ref[:, hidden : 2 * hidden], up_ref[:, cols])
+        row_grad = row_grad + dot_nt(mixed_ref[:, 2 * hidden :], router_ref[cols, :])
+        rb[slot, :, cols] = row_grad.astype(jnp.bfloat16)
+        ob[slot, :, cols] = dot_nn(act_ref[...], down_ref[:, cols]).astype(jnp.bfloat16)
+        return carry
+
+    lax.fori_loop(0, width // out_tile, width_step, 0)
+    for j in range(pair_count):
+        @pl.when(step == j)
+        def _(j=j):
+            for copy in stores(2 * j, slot):
+                copy.start()
+
+    @pl.when(step == pair_count - 1)
+    def _():
+        for copy in stores(0, slot):
+            copy.wait()
+        if pair_count > 1:
+            for copy in stores(0, 1 - slot):
+                copy.wait()
+
+
+def expert_call(xs, cs, code, router, gate_mat, up_mat, down_mat, local_experts):
+    count = len(xs)
+    pair_count = count // 2
+    rows, width = xs[0].shape
+    hidden = gate_mat.shape[0]
+    lane_pad = router.shape[1]
+    span = 2 * rows
+    mixed_width = 2 * hidden + lane_pad
+    any_spec = pl.BlockSpec(memory_space=pl.ANY)
+    whole = lambda shape: pl.BlockSpec(shape, lambda i: (0, 0), pipeline_mode=pl.Buffered(1))
+    block = jax.ShapeDtypeStruct((rows, width), jnp.bfloat16)
+    flops = 2 * span * pair_count * (width * hidden * 6 + width * lane_pad * 2)
+    results = pl.pallas_call(
+        functools.partial(expert_kernel, pair_count, local_experts, lane_pad),
+        grid=(pair_count,),
+        out_shape=[block] * (2 * count)
+        + [
+            jax.ShapeDtypeStruct((span * pair_count, mixed_width), jnp.bfloat16),
+            jax.ShapeDtypeStruct((span * pair_count, hidden), jnp.bfloat16),
+        ],
+        in_specs=[any_spec] * (2 * count)
+        + [
+            pl.BlockSpec((1, span, lane_pad), lambda i: (i, 0, 0)),
+            whole((width, lane_pad)),
+            whole((hidden, width)),
+            whole((hidden, width)),
+            whole((hidden, width)),
+        ],
+        out_specs=[any_spec] * (2 * count)
+        + [
+            pl.BlockSpec((span, mixed_width), lambda i: (i, 0)),
+            pl.BlockSpec((span, hidden), lambda i: (i, 0)),
+        ],
+        scratch_shapes=[
+            pltpu.VMEM((2, span, width), jnp.bfloat16),
+            pltpu.VMEM((2, span, width), jnp.bfloat16),
+            pltpu.VMEM((2, span, width), jnp.bfloat16),
+            pltpu.VMEM((2, span, width), jnp.bfloat16),
+            pltpu.VMEM((span, hidden), jnp.bfloat16),
+            pltpu.SemaphoreType.DMA((2, 4)),
+            pltpu.SemaphoreType.DMA((2, 4)),
+        ],
+        compiler_params=pltpu.CompilerParams(
+            dimension_semantics=("arbitrary",), vmem_limit_bytes=60 * 1024 * 1024
+        ),
+        cost_estimate=pl.CostEstimate(
+            flops=flops,
+            bytes_accessed=count * rows * width * 8 + 6 * hidden * width,
+            transcendentals=span * pair_count * hidden,
+        ),
+        name="experts",
+    )(*xs, *cs, code, router, gate_mat, up_mat, down_mat)
+    return results[:count], results[count : 2 * count], results[2 * count], results[2 * count + 1]
+
+
+def gathered(
+    tokens,
+    segments,
+    prefix,
+    expert_ids,
+    first_gain,
+    query_weight,
+    key_matrix,
+    value_matrix,
+    query_gain,
+    key_gain,
+    output_weight,
+    second_gain,
+    router,
+    gate_weight,
+    up_weight,
+    down_weight,
+    cotangent,
+):
+    low = jnp.bfloat16
+    full = jnp.float32
+    tp_count = lax.axis_size("tp")
+    fsdp_count = lax.axis_size("fsdp")
+    tp_rank = lax.axis_index("tp")
+    fsdp_rank = lax.axis_index("fsdp")
+    own_rows, model_dim = tokens.shape
+    seq_len = own_rows * tp_count
+    head_dim = fsdp_count * query_gain.shape[0]
+    query_count = query_weight.shape[1] // head_dim
+    kv_count = key_matrix.shape[1] // head_dim
+    score_scale = head_dim ** (-0.5)
+    local_experts, hidden_units = gate_weight.shape[:2]
+    expert_total = fsdp_count * local_experts
+    top_count = expert_ids.shape[1]
+    capacity = (9 * top_count * seq_len + 8 * expert_total - 1) // (8 * expert_total)
+
+    token_blocks = tp_gather(tokens)
+    wide_shard = jnp.concatenate([query_weight, key_matrix, value_matrix], axis=1)
+    wide_all = lax.all_gather(wide_shard, "fsdp", axis=0, tiled=True)
+    gains = lax.all_gather(
+        jnp.concatenate([first_gain, second_gain, query_gain, key_gain]), "fsdp", axis=0
+    )
+    gain_one = gains[:, : first_gain.shape[0]].reshape(-1).astype(full)
+    gains = gains[:, first_gain.shape[0] :]
+    gain_two = gains[:, : second_gain.shape[0]].reshape(-1).astype(full)
+    gains = gains[:, second_gain.shape[0] :]
+    gain_query = gains[:, : query_gain.shape[0]].reshape(-1).astype(full)
+    gain_key = gains[:, query_gain.shape[0] :].reshape(-1).astype(full)
+    router_all = lax.all_gather(router, "fsdp", axis=0, tiled=True)
+    output_all = lax.all_gather(output_weight, "fsdp", axis=0, tiled=True)
+
+    lanes = jnp.arange(expert_total, dtype=jnp.int32)
+    picked = jnp.sum((expert_ids[:, :, None] == lanes[None, None, :]).astype(full), axis=1)
+    order = jnp.arange(seq_len, dtype=jnp.int32)
+    before = (order[None, :] < order[:, None]).astype(low)
+    earlier = jnp.dot(before, picked.astype(low), preferred_element_type=full)
+    code = (picked * (1.0 + (earlier < capacity).astype(full))).astype(low)
+    code = xor_order(code.reshape(tp_count, own_rows, expert_total), tp_rank, 0)
+    codes = jnp.swapaxes(code, 1, 2)[None]
+    for mask in (1, 2, 4):
+        codes = jnp.concatenate([codes, swap(codes, "fsdp", mask)], axis=0)
+    shift = fsdp_rank * local_experts
+    codes = jnp.concatenate([codes, codes], axis=2)
+    codes = jnp.swapaxes(lax.dynamic_slice_in_dim(codes, shift, expert_total, 2), 2, 3)
+    lane_pad = 128
+    codes = jnp.pad(codes, ((0, 0), (0, 0), (0, 0), (0, lane_pad - expert_total)))
+    router_near = jnp.concatenate([router_all, router_all], axis=1)
+    router_near = lax.dynamic_slice_in_dim(router_near, shift, expert_total, 1)
+    router_near = jnp.pad(router_near, ((0, 0), (0, lane_pad - expert_total)))
+
+    cotangent_blocks = tp_gather(cotangent)
+    cotangent_near = [plane_gather(b, r % 2 == 1) for r, b in enumerate(cotangent_blocks)]
+
+    segment_row = xor_order(segments[0].reshape(tp_count, own_rows), tp_rank, 0).reshape(-1)
+    token_pos = xor_order(order.reshape(tp_count, own_rows), tp_rank, 0).reshape(-1)
+    prefix_len = prefix[0]
+    doc_start = jnp.sum((segment_row[None, :] < segment_row[:, None]).astype(jnp.int32), axis=1)
+    cos_table, sin_table = turned_tables(token_pos - doc_start, head_dim)
+
+    seq_rows = jnp.concatenate(token_blocks, axis=0)
+    input_hat, input_inverse = norm_forward(seq_rows.astype(full))
+    first_normed = (input_hat * gain_one).astype(low)
+    wide_pre = jnp.dot(first_normed, wide_all, preferred_element_type=full)
+    query_cols = query_count * head_dim
+    kv_cols = kv_count * head_dim
+    query_pre = wide_pre[:, :query_cols].reshape(seq_len, query_count, head_dim)
+    key_pre = wide_pre[:, query_cols : query_cols + kv_cols].reshape(seq_len, kv_count, head_dim)
+    value_heads = wide_pre[:, query_cols + kv_cols :].astype(low).reshape(seq_len, kv_count, head_dim)
+    query_hat, query_inverse = norm_forward(query_pre)
+    key_hat, key_inverse = norm_forward(key_pre)
+    query_heads = rotate(query_hat * gain_query, cos_table, sin_table).astype(low)
+    key_heads = rotate(key_hat * gain_key, cos_table, sin_table).astype(low)
+    span = min(512, seq_len)
+    starts = jnp.arange(seq_len // span, dtype=jnp.int32) * span
+    mixed_rows, log_totals = lax.map(
+        lambda begin: forward_block(
+            begin, query_heads, key_heads, value_heads, segment_row, token_pos, prefix_len, span, score_scale
+        ),
+        starts,
+    )
+    mixed_low = mixed_rows.reshape(seq_len, query_cols).astype(low)
+    attended_part = jnp.einsum("sa,da->sd", mixed_low, output_all, preferred_element_type=full).astype(low)
+    attended = tp_reduce([attended_part[r * own_rows : (r + 1) * own_rows] for r in range(tp_count)])
+    hidden = tokens.astype(full) + attended
+    hidden_hat, hidden_inverse = norm_forward(hidden)
+    normed_two = (hidden_hat * gain_two).astype(low)
+
+    normed_blocks = tp_gather(normed_two)
+    normed_near = [plane_gather(b, r % 2 == 1) for r, b in enumerate(normed_blocks)]
+    gate_mat = gate_weight.reshape(-1, model_dim)
+    up_mat = up_weight.reshape(-1, model_dim)
+    down_mat = down_weight.reshape(-1, model_dim)
+    row_sums, out_sums, mixed_grads, act_gates = [], [], [], []
+    for r in range(tp_count):
+        code_r = codes[:, r].reshape(fsdp_count // 2, 2 * own_rows, lane_pad)
+        row_parts, out_parts, mixed_grad, act_gate = expert_call(
+            normed_near[r], cotangent_near[r], code_r, router_near, gate_mat, up_mat, down_mat, local_experts
+        )
+        row_sums.append(plane_reduce(row_parts, r % 2 == 1))
+        out_sums.append(plane_reduce(out_parts, r % 2 == 1))
+        mixed_grads.append(mixed_grad)
+        act_gates.append(act_gate)
+    normed_two_grad = tp_reduce(row_sums)
+    output = (hidden + tp_reduce(out_sums)).astype(low)
+
+    flat = lambda near: jnp.concatenate([b for blocks in near for b in blocks], axis=0)
+    wide_grad = jnp.einsum(
+        "tf,td->fd", jnp.concatenate(mixed_grads, axis=0), flat(normed_near), preferred_element_type=full
+    )
+    down_grad = jnp.einsum(
+        "tf,td->fd", jnp.concatenate(act_gates, axis=0), flat(cotangent_near), preferred_element_type=full
+    )
+    flat_hidden = local_experts * hidden_units
+    gate_wgrad = wide_grad[:flat_hidden].reshape(gate_weight.shape)
+    up_wgrad = wide_grad[flat_hidden : 2 * flat_hidden].reshape(up_weight.shape)
+    down_wgrad = down_grad.reshape(down_weight.shape)
+    router_part = wide_grad[2 * flat_hidden : 2 * flat_hidden + expert_total]
+    router_part = jnp.concatenate([router_part, router_part], axis=0)
+    router_part = lax.dynamic_slice_in_dim(router_part, expert_total - shift, expert_total, 0).T
+
+    hidden_grad = cotangent.astype(full) + norm_back(normed_two_grad, hidden_hat, hidden_inverse, gain_two)
+    second_part = jnp.sum(normed_two_grad * hidden_hat, axis=0)
+    attended_grad = jnp.concatenate(tp_gather(hidden_grad.astype(low)), axis=0)
+    output_wgrad = jnp.einsum("sd,sa->da", attended_grad, mixed_low, preferred_element_type=full)
+    mixed_grad = jnp.dot(attended_grad, output_all, preferred_element_type=full).astype(low)
+    zero_heads = jnp.zeros((seq_len, kv_count, head_dim), full)
+    (key_turn_grad, value_grad), query_turn_grad = lax.scan(
+        lambda carried, inputs: backward_block(
+            carried,
+            inputs,
+            query_heads,
+            key_heads,
+            value_heads,
+            mixed_grad,
+            segment_row,
+            token_pos,
+            prefix_len,
+            span,
+            score_scale,
+        ),
+        (zero_heads, zero_heads),
+        (starts, log_totals),
+    )
+    query_turn_grad = query_turn_grad.reshape(seq_len, query_count, head_dim)
+    query_norm_grad = rotate_back(query_turn_grad, cos_table, sin_table)
+    key_norm_grad = rotate_back(key_turn_grad, cos_table, sin_table)
+    query_gain_part = jnp.sum(query_norm_grad * query_hat, axis=(0, 1))
+    key_gain_part = jnp.sum(key_norm_grad * key_hat, axis=(0, 1))
+    query_pre_grad = norm_back(query_norm_grad, query_hat, query_inverse, gain_query).astype(low)
+    key_pre_grad = norm_back(key_norm_grad, key_hat, key_inverse, gain_key).astype(low)
+    wide_pre_grad = jnp.concatenate(
+        [
+            query_pre_grad.reshape(seq_len, -1),
+            key_pre_grad.reshape(seq_len, -1),
+            value_grad.astype(low).reshape(seq_len, -1),
+        ],
+        axis=1,
+    )
+    wide_wgrad = jnp.einsum("sd,sa->da", first_normed, wide_pre_grad, preferred_element_type=full)
+    normed_one_part = jnp.einsum("sa,da->sd", wide_pre_grad, wide_all, preferred_element_type=full).astype(low)
+    normed_one_grad = tp_reduce([normed_one_part[r * own_rows : (r + 1) * own_rows] for r in range(tp_count)])
+    own_hat, own_inverse = norm_forward(tokens.astype(full))
+    first_part = jnp.sum(normed_one_grad * own_hat, axis=0)
+    input_grad = (hidden_grad + norm_back(normed_one_grad, own_hat, own_inverse, gain_one)).astype(low)
+
+    sizes = []
+    pieces = []
+    for part in (first_part, second_part, query_gain_part, key_gain_part, router_part):
+        part = part.reshape(fsdp_count, tp_count, -1)
+        sizes.append(part.shape[2])
+        pieces.append(part)
+    packed = jnp.concatenate(pieces, axis=2)
+    packed = small_reduce(xor_order(xor_order(packed, fsdp_rank, 0), tp_rank, 1))
+    small = []
+    begin = 0
+    for size in sizes:
+        small.append(packed[begin : begin + size])
+        begin += size
+    wide_wshard = lax.psum_scatter(wide_wgrad.astype(low), "fsdp", scatter_dimension=0, tiled=True).astype(full)
+    output_wshard = lax.psum_scatter(
+        output_wgrad.astype(low), "fsdp", scatter_dimension=0, tiled=True
+    ).astype(full)
+    return (
+        output,
+        input_grad,
+        small[0],
+        wide_wshard[:, :query_cols],
+        wide_wshard[:, query_cols : query_cols + kv_cols],
+        wide_wshard[:, query_cols + kv_cols :],
+        small[2],
+        small[3],
+        output_wshard,
+        small[1],
+        small[4].reshape(-1, expert_total),
         gate_wgrad,
         up_wgrad,
         down_wgrad,
@@ -560,7 +1046,7 @@
         P(("fsdp", "tp"), None),
     )
     return jax.shard_map(
-        local,
+        gathered if mesh.shape["fsdp"] == 8 and mesh.shape["tp"] == 4 else exchanged,
         mesh=mesh,
         in_specs=placed,
         out_specs=(

time: 3640 us -> 1860 us (0.51)
  waiting for transfers between devices: 1460 us -> 819 us
  other arithmetic: 610 us -> 120 us
  blocking collectives: 519 us -> 35.5 us
  local copies, waits for them, and re-layouts: 642 us -> 224 us
  Pallas kernels: 0 us -> 270 us
  matrix products: 340 us -> 238 us
  starting transfers between devices: 31.2 us -> 112 us
    all_to_all x4 -> x0, waiting for transfers between devices: 1180 us -> none  [the longest x2 817 us: to_experts(): lax.all_to_all(buffer, 'fsdp', split_axis=0, concat_axis=2, tiled=True)[0]]
    ppermute x0 -> x144, waiting for transfers between devices: none -> 819 us  [swap(): return lax.ppermute(values, axis, partners(lax.axis_size(axis), mask))]
    all_gather x5 -> x1, blocking collectives: 449 us -> 9.44 us  [gathered(): router_all = lax.all_gather(router, 'fsdp', axis=0, tiled=True)]
    pallas_call x0 -> x4, Pallas kernels: none -> 270 us  [expert_call(): pl.pallas_call(functools.partial(expert_kernel, pair_count, local_experts...]
    scatter-add x2 -> x0, other arithmetic: 237 us -> none  [the longest x1 118 us: local(): jax.ops.segment_sum(back_rows.astype(jnp.float32), slot_token, num_segmen...]
    gather x3 -> x0, local copies, waits for them, and re-layouts: 194 us -> none  [the longest x1 72 us: local(): slot_rows = grad_pad[slot_token]]
    reduce_scatter x7 -> x2, waiting for transfers between devices: 118 us -> 0.01 us  [the longest x1 0.01 us: gathered(): lax.psum_scatter(wide_wgrad.astype(low), 'fsdp', scatter_dimension=0, til...]
    ppermute x0 -> x144, starting transfers between devices: none -> 112 us  [swap(): return lax.ppermute(values, axis, partners(lax.axis_size(axis), mask))]
  transfers between devices with their start and end apart: 17 -> 148, of which waited for: 8 -> 51; matrix products, arithmetic and copies ran while one was open for 20% -> 30% of each run, Pallas kernels for 0% -> 15%
where the time goes in v1:
time: 1860 us; the launch traced here: 1850 us
  waiting for transfers between devices  819 us (44%)
  Pallas kernels  270 us (15%)
  matrix products  238 us (13%)
  local copies, waits for them, and re-layouts  224 us (12%)
  other arithmetic  120 us (6%)
  starting transfers between devices  112 us (6%)
  blocking collectives  35.5 us (2%)
    ppermute x144, waiting for transfers between devices, swap(): return lax.ppermute(values, axis, partners(lax.axis_size(axis), mask))  819 us
    pallas_call x4, Pallas kernels, expert_call(): pl.pallas_call(functools.partial(expert_kernel, pair_count, local_experts...  270 us
    unnamed x414, local copies, waits for them, and re-layouts  130 us
    ppermute x144, starting transfers between devices, swap(): return lax.ppermute(values, axis, partners(lax.axis_size(axis), mask))  112 us
    dot_general x1, matrix products, gathered(): jnp.einsum('tf,td->fd', jnp.concatenate(mixed_grads, axis=0), flat(normed...  71.4 us
    dot_general x1, matrix products, gathered(): jnp.einsum('tf,td->fd', jnp.concatenate(act_gates, axis=0), flat(cotangen...  42.1 us
  transfers between devices with their start and end apart: 148, of which 51 were waited for; matrix products, arithmetic and copies ran while one was open for 30% of the time, Pallas kernels for 15%

profile of v1, /device:TPU:0, one launch (start us, length us, event | category | flops | bytes accessed | tf_op | source)
XLA Modules:
  0.0 1845.1 jit_solution(7911124311168559916)
XLA Ops:
  22.3 26.0 %all-reduce.2 = bf16[4352]{0:T(1024)(128)(2,1)S(1)} all-reduce(bf16[4352]{0:T(1024)(128)(2,1)S(1)} %dynamic-update-slice), channel_id=2, replica_groups=mesh['fsdp'=8,'tp'=4] {'fsdp'}, use_global_device_ids=true, to_apply=%add.2 | all-reduce | flops 4352 | bytes 17408
  217.8 22.8 %collective-permute-done.88.refs_10_ = bf16[256,2048]{1,0:T(8,128)(2,1)} collective-permute-done((bf16[256,2048]{1,0:T(8,128)(2,1)}, bf16[256,2048]{1,0:T(8,128)(2,1)}, u32[]{:S(2)}, u32[]{:S(2)}) %collective-permute-start.88) | collective-permute-done | bytes 1048608 | tf_op jit(solution)/shard_map/ppermute | solution.py:564
  241.1 21.3 %collective-permute-done.68.refs_14_ = bf16[256,2048]{1,0:T(8,128)(2,1)} collective-permute-done((bf16[256,2048]{1,0:T(8,128)(2,1)}, bf16[256,2048]{1,0:T(8,128)(2,1)}, u32[]{:S(2)}, u32[]{:S(2)}) %collective-permute-start.68) | collective-permute-done | bytes 1048608 | tf_op jit(solution)/shard_map/ppermute | solution.py:564
  296.2 42.0 %while.27 = (s32[]{:T(128)}, bf16[2,512,1024]{2,1,0:T(8,128)(2,1)}, f32[2,1,8,512]{3,2,1,0:T(8,128)S(1)}, s32[2]{0:T(128)S(1)}, s32[1024]{0:T(1024)S(1)}, /*inde...) while((s32[]{:T(128)}, bf16[2,512,1024]{2,1,0:T(8,128)(2,1)}, ...), condition=%wide.region_7.8_spmd, body=%wide.region_4.7_spmd.sunk | while | flops 2195715072 | bytes 59418840 | solution.py:902
  382.8 23.9 %collective-permute-done.5 = bf16[256,2048]{1,0:T(8,128)(2,1)S(1)} collective-permute-done((bf16[256,2048]{1,0:T(8,128)(2,1)S(1)}, bf16[256,2048]{1,0:T(8,128)(2,1)S(1)}, u32[]{:S(2)}, u32[]{:S(2)}) %collective-permute-start.5) | collective-permute-done | bytes 1048608 | tf_op jit(solution)/shard_map/ppermute | solution.py:564
  406.7 44.8 %collective-permute-done.4 = bf16[256,2048]{1,0:T(8,128)(2,1)S(1)} collective-permute-done((bf16[256,2048]{1,0:T(8,128)(2,1)S(1)}, bf16[256,2048]{1,0:T(8,128)(2,1)S(1)}, u32[]{:S(2)}, u32[]{:S(2)}) %collective-permute-start.4) | collective-permute-done | bytes 1048608 | tf_op jit(solution)/shard_map/ppermute | solution.py:564
  488.0 25.4 %collective-permute-done.30.refs_0_ = bf16[256,2048]{1,0:T(8,128)(2,1)S(1)} collective-permute-done((bf16[256,2048]{1,0:T(8,128)(2,1)S(1)}, bf16[256,2048]{1,0:T(8,128)(2,1)S(1)}, u32[]{:S(2)}, u32[]{:S(2)}) %collective-permute-start.30) | collective-permute-done | bytes 1048608 | tf_op jit(solution)/shard_map/ppermute | solution.py:564
  521.5 54.7 %collective-permute-done.54.refs_0_ = bf16[256,2048]{1,0:T(8,128)(2,1)} collective-permute-done((bf16[256,2048]{1,0:T(8,128)(2,1)S(1)}, bf16[256,2048]{1,0:T(8,128)(2,1)}, u32[]{:S(2)}, u32[]{:S(2)}) %collective-permute-start.54) | collective-permute-done | bytes 1048608 | tf_op jit(solution)/shard_map/ppermute | solution.py:564
  579.8 67.6 %experts.4 = (bf16[256,2048]{1,0:T(8,128)(2,1)}, bf16[256,2048]{1,0:T(8,128)(2,1)}, bf16[256,2048]{1,0:T(8,128)(2,1)}, bf16[256,2048]{1,0:T(8,128)(2,1)}, bf16[2...) custom-call(bf16[256,2048]{1,0:T(8,128)(2,1)} %copy-done.57, ...), custom_call_target="tpu_custom_call" | custom-call | flops 40802189312 | bytes 42991616 | tf_op jit(solution)/shard_map/experts/pallas_call | solution.py:765
  680.2 22.5 %collective-permute-done.56.refs_2_ = bf16[256,2048]{1,0:T(8,128)(2,1)} collective-permute-done((bf16[256,2048]{1,0:T(8,128)(2,1)}, bf16[256,2048]{1,0:T(8,128)(2,1)}, u32[]{:S(2)}, u32[]{:S(2)}) %collective-permute-start.56) | collective-permute-done | bytes 1048608 | tf_op jit(solution)/shard_map/ppermute | solution.py:564
  724.5 67.3 %experts.5 = (bf16[256,2048]{1,0:T(8,128)(2,1)}, bf16[256,2048]{1,0:T(8,128)(2,1)}, bf16[256,2048]{1,0:T(8,128)(2,1)}, bf16[256,2048]{1,0:T(8,128)(2,1)}, bf16[2...) custom-call(bf16[256,2048]{1,0:T(8,128)(2,1)} %copy-done.82, ...), custom_call_target="tpu_custom_call" | custom-call | flops 40802189312 | bytes 42991616 | tf_op jit(solution)/shard_map/experts/pallas_call | solution.py:765
  795.3 67.7 %experts.6 = (bf16[256,2048]{1,0:T(8,128)(2,1)}, bf16[256,2048]{1,0:T(8,128)(2,1)}, bf16[256,2048]{1,0:T(8,128)(2,1)}, bf16[256,2048]{1,0:T(8,128)(2,1)}, bf16[2...) custom-call(bf16[256,2048]{1,0:T(8,128)(2,1)} %collective-permute-do, ...), custom_call_target="tpu_custom_call" | custom-call | flops 40802189312 | bytes 42991616 | tf_op jit(solution)/shard_map/experts/pallas_call | solution.py:765
  874.6 67.4 %experts.7 = (bf16[256,2048]{1,0:T(8,128)(2,1)}, bf16[256,2048]{1,0:T(8,128)(2,1)}, bf16[256,2048]{1,0:T(8,128)(2,1)}, bf16[256,2048]{1,0:T(8,128)(2,1)}, bf16[2...) custom-call(bf16[256,2048]{1,0:T(8,128)(2,1)} %copy-done.80, ...), custom_call_target="tpu_custom_call" | custom-call | flops 40802189312 | bytes 42991616 | tf_op jit(solution)/shard_map/experts/pallas_call | solution.py:765
  972.4 22.1 %collective-permute-done.28 = bf16[256,2048]{1,0:T(8,128)(2,1)S(1)} collective-permute-done((bf16[256,2048]{1,0:T(8,128)(2,1)S(1)}, bf16[256,2048]{1,0:T(8,128)(2,1)S(1)}, u32[]{:S(2)}, u32[]{:S(2)}) %collective-permute-start.28) | collective-permute-done | bytes 1048608 | tf_op jit(solution)/shard_map/ppermute | solution.py:564
  1025.5 21.0 %collective-permute-done.128 = bf16[256,2048]{1,0:T(8,128)(2,1)S(1)} collective-permute-done((bf16[256,2048]{1,0:T(8,128)(2,1)S(1)}, bf16[256,2048]{1,0:T(8,128)(2,1)S(1)}, u32[]{:S(2)}, u32[]{:S(2)}) %collective-permute-start.128) | collective-permute-done | bytes 1048608 | tf_op jit(solution)/shard_map/ppermute | solution.py:564
  1076.8 21.2 %collective-permute-done.112 = bf16[256,2048]{1,0:T(8,128)(2,1)S(1)} collective-permute-done((bf16[256,2048]{1,0:T(8,128)(2,1)S(1)}, bf16[256,2048]{1,0:T(8,128)(2,1)S(1)}, u32[]{:S(2)}, u32[]{:S(2)}) %collective-permute-start.112) | collective-permute-done | bytes 1048608 | tf_op jit(solution)/shard_map/ppermute | solution.py:564
  1121.5 20.7 %collective-permute-done.131 = bf16[256,2048]{1,0:T(8,128)(2,1)S(1)} collective-permute-done((bf16[256,2048]{1,0:T(8,128)(2,1)S(1)}, bf16[256,2048]{1,0:T(8,128)(2,1)S(1)}, u32[]{:S(2)}, u32[]{:S(2)}) %collective-permute-start.131) | collective-permute-done | bytes 1048608 | tf_op jit(solution)/shard_map/ppermute | solution.py:564
  1169.4 21.4 %collective-permute-done.123 = bf16[256,2048]{1,0:T(8,128)(2,1)S(1)} collective-permute-done((bf16[256,2048]{1,0:T(8,128)(2,1)S(1)}, bf16[256,2048]{1,0:T(8,128)(2,1)S(1)}, u32[]{:S(2)}, u32[]{:S(2)}) %collective-permute-start.123) | collective-permute-done | bytes 1048608 | tf_op jit(solution)/shard_map/ppermute | solution.py:564
  1260.4 78.0 %collective-permute-done.124 = bf16[256,2048]{1,0:T(8,128)(2,1)S(1)} collective-permute-done((bf16[256,2048]{1,0:T(8,128)(2,1)S(1)}, bf16[256,2048]{1,0:T(8,128)(2,1)S(1)}, u32[]{:S(2)}, u32[]{:S(2)}) %collective-permute-start.124) | collective-permute-done | bytes 1048608 | tf_op jit(solution)/shard_map/ppermute | solution.py:564
  1346.1 45.7 %collective-permute-done.77 = bf16[256,2048]{1,0:T(8,128)(2,1)S(1)} collective-permute-done((bf16[256,2048]{1,0:T(8,128)(2,1)S(1)}, bf16[256,2048]{1,0:T(8,128)(2,1)S(1)}, u32[]{:S(2)}, u32[]{:S(2)}) %collective-permute-start.77) | collective-permute-done | bytes 1048608 | tf_op jit(solution)/shard_map/ppermute | solution.py:564
  1423.0 59.6 %collective-permute-done.134 = bf16[256,2048]{1,0:T(8,128)(2,1)S(1)} collective-permute-done((bf16[256,2048]{1,0:T(8,128)(2,1)S(1)}, bf16[256,2048]{1,0:T(8,128)(2,1)S(1)}, u32[]{:S(2)}, u32[]{:S(2)}) %collective-permute-start.134) | collective-permute-done | bytes 1048608 | tf_op jit(solution)/shard_map/ppermute | solution.py:564
  1499.6 93.2 %while.28 = (s32[]{:T(128)}, f32[1024,1,128]{0,2,1:T(8,128)}, f32[1024,1,128]{0,2,1:T(8,128)}, f32[2,512,8,128]{3,2,1,0:T(8,128)}, s32[2]{0:T(128)S(1)}, /*index...) while((s32[]{:T(128)}, f32[1024,1,128]{0,2,1:T(8,128)}, ...), condition=%wide.region_14.15_spmd.clone, body=%wide.region_12.14_spmd.clone.sunk | while | flops 5409731584 | bytes 191818288 | solution.py:954
  1637.7 71.4 %fusion.38 = f32[1664,2048]{1,0:T(8,128)} fusion(bf16[8192,2048]{1,0:T(8,128)(2,1)} %constant_dynamic-update-slice_fusion.1, bf16[2048,1664]{1,0:T(8,128)(2,1)} %get-tuple-element.300, bf16[2048,1664]{1,0:T(8,128)(2,1)} %get-tuple-element.299, bf16[2048,1664]{1,0:T(8,128)(2,1)} %get-tuple-element.298, bf16[2048,1664]{1,0:T(8,128)(2,1)} %get-tuple-element.297), kind=kOutput, calls=%fused_computation.51 | convolution fusion | flops 55943626752 | bytes 74448896 | tf_op jit(solution)/shard_map/tf,td->fd/dot_general | solution.py:934
  1764.9 42.1 %fusion.46 = f32[768,2048]{1,0:T(8,128)} fusion(bf16[8192,2048]{1,0:T(8,128)(2,1)} %constant_dynamic-update-slice_fusion.33, bf16[2048,768]{1,0:T(8,128)(2,1)} %get-tuple-element.304, bf16[2048,768]{1,0:T(8,128)(2,1)} %get-tuple-element.303, bf16[2048,768]{1,0:T(8,128)(2,1)} %get-tuple-element.302, bf16[2048,768]{1,0:T(8,128)(2,1)} %get-tuple-element.301), kind=kOutput, calls=%fused_computation.59 | convolution fusion | flops 25820135424 | bytes 52428800 | tf_op jit(solution)/shard_map/tf,td->fd/dot_general | solution.py:937
  (1016 shorter events, 904.2 us)
Async XLA Ops:
  7.3 258.6 %all-gather.4.cloned.1.call-start = ((), (), s32[]{:S(2)}) async-start(), calls=%async_computation.2 | async-start | bytes 5898240 | tf_op jit(solution)/shard_map/all_gather | solution.py:846
  9.4 328.8 %all-gather.6.cloned.1.call-start = ((), (), s32[]{:S(2)}) async-start(), calls=%async_computation.3 | async-start | bytes 4718592 | tf_op jit(solution)/shard_map/all_gather | solution.py:857
  15.2 108.5 %collective-permute-start.2 = (bf16[256,2048]{1,0:T(8,128)(2,1)}, bf16[256,2048]{1,0:T(8,128)(2,1)}, u32[]{:S(2)}, u32[]{:S(2)}) collective-permute-start(bf16[256,2048]{1,0:T(8,128)(2,1)} %param.21), channel_id=1, source_target_pairs={{0,3},{1,2},{2,1},{3,0},{4,7},{5,6},{6,5},{7,4},{8,11},{9,10},{10,... | collective-permute-start | bytes 3145736 | tf_op jit(solution)/shard_map/ppermute | solution.py:564
  18.3 1814.2 %reduce-scatter.5.cloned.1.call-start = ((), (), s32[]{:S(2)}) async-start(), calls=%async_computation.5 | async-start | bytes 4718592 | tf_op jit(solution)/shard_map/reduce_scatter | solution.py:1007
  215.2 157.0 %collective-permute-start.90 = (bf16[256,2048]{1,0:T(8,128)(2,1)}, bf16[256,2048]{1,0:T(8,128)(2,1)}, u32[]{:S(2)}, u32[]{:S(2)}) collective-permute-start(bf16[256,2048]{1,0:T(8,128)(2,1)} %collective-permute-done.86.refs_8_), channel_id=1, source_target_pairs={{0,16},{4,20},{8,24},{12,28},{16,0},{20,4},{24,8},{28,12},{1,17},{... | collective-permute-start | bytes 3145736 | tf_op jit(solution)/shard_map/ppermute | solution.py:564
  240.5 106.1 %collective-permute-start.67 = (bf16[256,2048]{1,0:T(8,128)(2,1)}, bf16[256,2048]{1,0:T(8,128)(2,1)}, u32[]{:S(2)}, u32[]{:S(2)}) collective-permute-start(bf16[256,2048]{1,0:T(8,128)(2,1)} %collective-permute-done.66.refs_12_), channel_id=1, source_target_pairs={{0,4},{4,0},{8,12},{12,8},{16,20},{20,16},{24,28},{28,24},{1,5},{5... | collective-permute-start | bytes 3145736 | tf_op jit(solution)/shard_map/ppermute | solution.py:564
  240.6 131.7 %collective-permute-start.92 = (bf16[256,2048]{1,0:T(8,128)(2,1)}, bf16[256,2048]{1,0:T(8,128)(2,1)}, u32[]{:S(2)}, u32[]{:S(2)}) collective-permute-start(bf16[256,2048]{1,0:T(8,128)(2,1)} %collective-permute-done.88.refs_10_), channel_id=1, source_target_pairs={{0,16},{4,20},{8,24},{12,28},{16,0},{20,4},{24,8},{28,12},{1,17},{... | collective-permute-start | bytes 3145736 | tf_op jit(solution)/shard_map/ppermute | solution.py:564
  240.9 118.1 %collective-permute-start.65 = (bf16[256,2048]{1,0:T(8,128)(2,1)}, bf16[256,2048]{1,0:T(8,128)(2,1)}, u32[]{:S(2)}, u32[]{:S(2)}) collective-permute-start(bf16[256,2048]{1,0:T(8,128)(2,1)} %collective-permute-done.64.refs_10_), channel_id=1, source_target_pairs={{0,4},{4,0},{8,12},{12,8},{16,20},{20,16},{24,28},{28,24},{1,5},{5... | collective-permute-start | bytes 3145736 | tf_op jit(solution)/shard_map/ppermute | solution.py:564
  262.5 97.7 %collective-permute-start.69 = (bf16[256,2048]{1,0:T(8,128)(2,1)}, bf16[256,2048]{1,0:T(8,128)(2,1)}, u32[]{:S(2)}, u32[]{:S(2)}) collective-permute-start(bf16[256,2048]{1,0:T(8,128)(2,1)} %collective-permute-done.68.refs_14_), channel_id=1, source_target_pairs={{0,4},{4,0},{8,12},{12,8},{16,20},{20,16},{24,28},{28,24},{1,5},{5... | collective-permute-start | bytes 3145736 | tf_op jit(solution)/shard_map/ppermute | solution.py:564
  360.2 91.3 %collective-permute-start.4 = (bf16[256,2048]{1,0:T(8,128)(2,1)S(1)}, bf16[256,2048]{1,0:T(8,128)(2,1)S(1)}, u32[]{:S(2)}, u32[]{:S(2)}) collective-permute-start(bf16[256,2048]{1,0:T(8,128)(2,1)S(1)} %get-tuple-element.616), channel_id=1, source_target_pairs={{0,2},{1,3},{2,0},{3,1},{4,6},{5,7},{6,4},{7,5},{8,10},{9,11},{10,... | collective-permute-start | bytes 3145736 | tf_op jit(solution)/shard_map/ppermute | solution.py:564
  372.3 89.7 %collective-permute-start.89 = (bf16[256,2048]{1,0:T(8,128)(2,1)}, bf16[256,2048]{1,0:T(8,128)(2,1)S(1)}, u32[]{:S(2)}, u32[]{:S(2)}) collective-permute-start(bf16[256,2048]{1,0:T(8,128)(2,1)} %collective-permute-done.88.refs_10_), channel_id=1, source_target_pairs={{0,4},{4,0},{8,12},{12,8},{16,20},{20,16},{24,28},{28,24},{1,5},{5... | collective-permute-start | bytes 3145736 | tf_op jit(solution)/shard_map/ppermute | solution.py:564
  521.1 129.6 %collective-permute-start.31 = (bf16[256,2048]{1,0:T(8,128)(2,1)S(1)}, bf16[256,2048]{1,0:T(8,128)(2,1)}, u32[]{:S(2)}, u32[]{:S(2)}) collective-permute-start(bf16[256,2048]{1,0:T(8,128)(2,1)S(1)} %collective-permute-done.30.refs_0_), channel_id=1, source_target_pairs={{0,4},{4,0},{8,12},{12,8},{16,20},{20,16},{24,28},{28,24},{1,5},{5... | collective-permute-start | bytes 3145736 | tf_op jit(solution)/shard_map/ppermute | solution.py:564
  675.9 118.3 %collective-permute-start.55 = (bf16[256,2048]{1,0:T(8,128)(2,1)}, bf16[256,2048]{1,0:T(8,128)(2,1)}, u32[]{:S(2)}, u32[]{:S(2)}) collective-permute-start(bf16[256,2048]{1,0:T(8,128)(2,1)} %collective-permute-done.54.refs_0_), channel_id=1, source_target_pairs={{0,4},{4,0},{8,12},{12,8},{16,20},{20,16},{24,28},{28,24},{1,5},{5... | collective-permute-start | bytes 3145736 | tf_op jit(solution)/shard_map/ppermute | solution.py:564
  680.2 114.4 %collective-permute-start.59 = (bf16[256,2048]{1,0:T(8,128)(2,1)S(1)}, bf16[256,2048]{1,0:T(8,128)(2,1)}, u32[]{:S(2)}, u32[]{:S(2)}) collective-permute-start(bf16[256,2048]{1,0:T(8,128)(2,1)S(1)} %collective-permute-done.58.refs_4_), channel_id=1, source_target_pairs={{0,4},{4,0},{8,12},{12,8},{16,20},{20,16},{24,28},{28,24},{1,5},{5... | collective-permute-start | bytes 3145736 | tf_op jit(solution)/shard_map/ppermute | solution.py:564
  702.7 91.5 %collective-permute-start.84 = (bf16[256,2048]{1,0:T(8,128)(2,1)}, bf16[256,2048]{1,0:T(8,128)(2,1)}, u32[]{:S(2)}, u32[]{:S(2)}) collective-permute-start(bf16[256,2048]{1,0:T(8,128)(2,1)} %collective-permute-done.80.refs_2_), channel_id=1, source_target_pairs={{0,16},{4,20},{8,24},{12,28},{16,0},{20,4},{24,8},{28,12},{1,17},{... | collective-permute-start | bytes 3145736 | tf_op jit(solution)/shard_map/ppermute | solution.py:564
  794.8 203.1 %collective-permute-start.23 = (bf16[256,2048]{1,0:T(8,128)(2,1)}, bf16[256,2048]{1,0:T(8,128)(2,1)S(1)}, u32[]{:S(2)}, u32[]{:S(2)}) collective-permute-start(bf16[256,2048]{1,0:T(8,128)(2,1)} %get-tuple-element.230), channel_id=1, source_target_pairs={{0,4},{4,0},{8,12},{12,8},{16,20},{20,16},{24,28},{28,24},{1,5},{5... | collective-permute-start | bytes 3145736 | tf_op jit(solution)/shard_map/ppermute | solution.py:564
  874.0 97.3 %collective-permute-start.26 = (bf16[256,2048]{1,0:T(8,128)(2,1)}, bf16[256,2048]{1,0:T(8,128)(2,1)}, u32[]{:S(2)}, u32[]{:S(2)}) collective-permute-start(bf16[256,2048]{1,0:T(8,128)(2,1)} %get-tuple-element.234), channel_id=1, source_target_pairs={{0,4},{4,0},{8,12},{12,8},{16,20},{20,16},{24,28},{28,24},{1,5},{5... | collective-permute-start | bytes 3145736 | tf_op jit(solution)/shard_map/ppermute | solution.py:564
  1235.7 102.7 %collective-permute-start.124 = (bf16[256,2048]{1,0:T(8,128)(2,1)S(1)}, bf16[256,2048]{1,0:T(8,128)(2,1)S(1)}, u32[]{:S(2)}, u32[]{:S(2)}) collective-permute-start(bf16[256,2048]{1,0:T(8,128)(2,1)S(1)} %add_convert_fusion.6), channel_id=1, source_target_pairs={{0,2},{1,3},{2,0},{3,1},{4,6},{5,7},{6,4},{7,5},{8,10},{9,11},{10,... | collective-permute-start | bytes 3145736 | tf_op jit(solution)/shard_map/ppermute | solution.py:564
  1235.7 102.7 %collective-permute-start.116 = (bf16[256,2048]{1,0:T(8,128)(2,1)S(1)}, bf16[256,2048]{1,0:T(8,128)(2,1)S(1)}, u32[]{:S(2)}, u32[]{:S(2)}) collective-permute-start(bf16[256,2048]{1,0:T(8,128)(2,1)S(1)} %add_convert_fusion.12), channel_id=1, source_target_pairs={{0,1},{1,0},{2,3},{3,2},{4,5},{5,4},{6,7},{7,6},{8,9},{9,8},{10,11... | collective-permute-start | bytes 3145736 | tf_op jit(solution)/shard_map/ppermute | solution.py:564
  1240.4 105.6 %collective-permute-start.25 = (bf16[256,2048]{1,0:T(8,128)(2,1)S(1)}, bf16[256,2048]{1,0:T(8,128)(2,1)S(1)}, u32[]{:S(2)}, u32[]{:S(2)}) collective-permute-start(bf16[256,2048]{1,0:T(8,128)(2,1)S(1)} %add_convert_fusion.47), channel_id=1, source_target_pairs={{0,8},{4,12},{8,0},{12,4},{16,24},{20,28},{24,16},{28,20},{1,9},{5... | collective-permute-start | bytes 3145736 | tf_op jit(solution)/shard_map/ppermute | solution.py:564
  1256.7 89.4 %collective-permute-start.29 = (bf16[256,2048]{1,0:T(8,128)(2,1)S(1)}, bf16[256,2048]{1,0:T(8,128)(2,1)S(1)}, u32[]{:S(2)}, u32[]{:S(2)}) collective-permute-start(bf16[256,2048]{1,0:T(8,128)(2,1)S(1)} %add_convert_fusion.44), channel_id=1, source_target_pairs={{0,16},{4,20},{8,24},{12,28},{16,0},{20,4},{24,8},{28,12},{1,17},{... | collective-permute-start | bytes 3145736 | tf_op jit(solution)/shard_map/ppermute | solution.py:564
  1257.7 88.3 %collective-permute-start.101 = (bf16[256,2048]{1,0:T(8,128)(2,1)S(1)}, bf16[256,2048]{1,0:T(8,128)(2,1)S(1)}, u32[]{:S(2)}, u32[]{:S(2)}) collective-permute-start(bf16[256,2048]{1,0:T(8,128)(2,1)S(1)} %add_convert_fusion.25), channel_id=1, source_target_pairs={{0,3},{1,2},{2,1},{3,0},{4,7},{5,6},{6,5},{7,4},{8,11},{9,10},{10,... | collective-permute-start | bytes 3145736 | tf_op jit(solution)/shard_map/ppermute | solution.py:564
  1490.9 343.7 %reduce-scatter.3.cloned.1.call-start = ((), (), s32[]{:S(2)}) async-start(), calls=%async_computation.4 | async-start | bytes 5898240 | tf_op jit(solution)/shard_map/reduce_scatter | solution.py:1006
  1636.5 89.6 %collective-permute-start.137 = (bf16[256,2048]{1,0:T(8,128)(2,1)}, bf16[256,2048]{1,0:T(8,128)(2,1)}, u32[]{:S(2)}, u32[]{:S(2)}) collective-permute-start(bf16[256,2048]{1,0:T(8,128)(2,1)} %get-tuple-element.611), channel_id=1, source_target_pairs={{0,2},{1,3},{2,0},{3,1},{4,6},{5,7},{6,4},{7,5},{8,10},{9,11},{10,... | collective-permute-start | bytes 3145736 | tf_op jit(solution)/shard_map/ppermute | solution.py:564
  (307 other events, 9365.9 us)
Sparse Core Ops, SparseCore 0:
  10.5 44.2 all-gather.3
  56.7 53.0 all-gather.5
  1491.0 50.5 reduce-scatter.4
  1763.6 56.0 reduce-scatter.2

commit v2 on v1

--- a/solution.py
+++ b/solution.py
@@ -576,14 +576,19 @@
     return values
 
 
-def plane_gather(block, odd):
-    side = swap(block, "fsdp", 2)
-    above = swap(block, "fsdp", 4)
-    corner = swap(side, "fsdp", 4) if odd else swap(above, "fsdp", 2)
-    gathered = []
-    for held in (block, side, above, corner):
-        gathered += [held, swap(held, "fsdp", 1)]
-    return gathered
+def chip_groups():
+    count = lax.axis_size("fsdp")
+    return [list(range(core, count, 2)) for core in range(2)]
+
+
+def exchange(parts):
+    return lax.all_to_all(
+        parts, "fsdp", split_axis=0, concat_axis=0, tiled=True, axis_index_groups=chip_groups()
+    )
+
+
+def plane_gather(block):
+    return exchange(jnp.broadcast_to(block[None], (lax.axis_size("fsdp") // 2, *block.shape)))
 
 
 def add_low(*terms):
@@ -593,16 +598,10 @@
     return total
 
 
-def plane_reduce(parts, odd):
+def plane_reduce(terms):
     low = jnp.bfloat16
-    own, side, above, corner = [
-        add_low(parts[m], swap(parts[m + 1], "fsdp", 1)).astype(low) for m in (0, 2, 4, 6)
-    ]
-    if odd:
-        side = add_low(side, swap(corner, "fsdp", 4)).astype(low)
-    else:
-        above = add_low(above, swap(corner, "fsdp", 2)).astype(low)
-    return add_low(own, swap(side, "fsdp", 2), swap(above, "fsdp", 4)).astype(low)
+    both = add_low(terms[0], swap(terms[1], "fsdp", 1)).astype(low)
+    return jnp.sum(exchange(both).astype(jnp.float32), axis=0).astype(low)
 
 
 def tp_gather(block):
@@ -628,61 +627,40 @@
     angles = jnp.concatenate([angles, angles], axis=1)
     return (jnp.cos(angles)[:, None, :], jnp.sin(angles)[:, None, :])
 
-
 def dot_nn(a, b):
     return lax.dot_general(a, b, (((1,), (0,)), ((), ())), preferred_element_type=jnp.float32)
 
+
 def dot_nt(a, b):
     return lax.dot_general(a, b, (((1,), (1,)), ((), ())), preferred_element_type=jnp.float32)
 
-def expert_kernel(pair_count, local_experts, lane_pad, *refs):
-    count = 2 * pair_count
-    x_refs, refs = refs[:count], refs[count:]
-    c_refs, refs = refs[:count], refs[count:]
-    code_ref, router_ref, gate_ref, up_ref, down_ref = refs[:5]
-    refs = refs[5:]
-    row_refs, refs = refs[:count], refs[count:]
-    out_refs, refs = refs[:count], refs[count:]
-    mixed_ref, act_ref, xb, cb, rb, ob, prod, in_sem, out_sem = refs
-    rows = x_refs[0].shape[0]
-    span = 2 * rows
+
+def expert_kernel(local_experts, kept_count, where_ref, *refs):
+    x_refs, c_refs, code_refs = refs[0:2], refs[2:4], refs[4:6]
+    router_ref, gate_ref, up_ref, down_ref = refs[6:10]
+    refs = refs[10 + kept_count :]
+    row_refs, out_refs, all_refs = refs[0:2], refs[2:4], refs[4:7]
+    mixed_ref, act_ref, prod, sem = refs[7:]
+    rows = x_refs[0].shape[1]
     hidden, width = gate_ref.shape
+    lane_pad = router_ref.shape[0]
     per_expert = hidden // local_experts
     step = pl.program_id(0)
-    slot = lax.rem(step, 2)
-
-    def loads(index, at):
-        for k in range(2):
-            where = pl.ds(k * rows, rows)
-            yield pltpu.make_async_copy(x_refs[index + k], xb.at[at, where], in_sem.at[at, 2 * k])
-            yield pltpu.make_async_copy(c_refs[index + k], cb.at[at, where], in_sem.at[at, 2 * k + 1])
-
-    def stores(index, at):
-        for k in range(2):
-            where = pl.ds(k * rows, rows)
-            yield pltpu.make_async_copy(rb.at[at, where], row_refs[index + k], out_sem.at[at, 2 * k])
-            yield pltpu.make_async_copy(ob.at[at, where], out_refs[index + k], out_sem.at[at, 2 * k + 1])
-
-    def start_loads(which, at):
-        for j in range(pair_count):
-            @pl.when(which == j)
-            def _(j=j):
-                for copy in loads(2 * j, at):
-                    copy.start()
-
-    @pl.when(step == 0)
-    def _():
-        start_loads(step, 0)
-
-    @pl.when(step + 1 < pair_count)
-    def _():
-        start_loads(step + 1, 1 - slot)
-
-    for copy in loads(0, slot):
-        copy.wait()
-
-    logits = dot_nn(xb[slot], router_ref[...])
-    code = code_ref[0].astype(jnp.float32)
+    core, block = where_ref[0], where_ref[1]
+
+    def keep(which, k):
+        source = (x_refs[k].at[0], mixed_ref.at[pl.ds(k * rows, rows)], act_ref.at[pl.ds(k * rows, rows)])[which]
+        owner = 2 * step + (core if k == 0 else 1 - core)
+        return pltpu.make_async_copy(source, all_refs[which].at[owner, block], sem.at[which, k])
+
+    for k in range(2):
+        keep(0, k).start()
+    logits, codes = [], []
+    for k in range(2):
+        logits.append(dot_nt(x_refs[k][0], router_ref[...]))
+        codes.append(code_refs[k][0, 0].astype(jnp.float32))
+    logits = jnp.concatenate(logits, axis=0)
+    code = jnp.concatenate(codes, axis=0)
     chosen = code > 0.5
     top = jnp.max(jnp.where(chosen, logits, -1e30), axis=1, keepdims=True)
     powers = jnp.where(chosen, jnp.exp(logits - top), 0.0)
@@ -693,9 +671,10 @@
     def hidden_step(j, carry):
         at = pl.multiple_of(j * tile, tile)
         cols = pl.ds(at, tile)
-        gate = dot_nt(xb[slot], gate_ref[cols, :])
-        up = dot_nt(xb[slot], up_ref[cols, :])
-        act_grad = dot_nt(cb[slot], down_ref[cols, :])
+        both = lambda sides, matrix: jnp.concatenate([dot_nt(sides[k][0], matrix) for k in range(2)], axis=0)
+        gate = both(x_refs, gate_ref[cols, :])
+        up = both(x_refs, up_ref[cols, :])
+        act_grad = both(c_refs, down_ref[cols, :])
         column = at + lax.broadcasted_iota(jnp.int32, (1, tile), 1)
         weight = kept[:, 0:1]
         for e in range(1, local_experts):
@@ -711,98 +690,81 @@
         return carry
 
     lax.fori_loop(0, hidden // tile, hidden_step, 0)
+    for k in range(2):
+        keep(2, k).start()
     owner = lax.broadcasted_iota(jnp.int32, (hidden, lane_pad), 0)
     lane = lax.broadcasted_iota(jnp.int32, (hidden, lane_pad), 1) * per_expert
     member = jnp.where((owner >= lane) & (owner < lane + per_expert), 1.0, 0.0).astype(jnp.bfloat16)
     weighted = dot_nn(prod[...], member)
     total = jnp.sum(weighted, axis=1, keepdims=True)
     mixed_ref[:, 2 * hidden :] = (weighted - probs * total).astype(jnp.bfloat16)
-
-    @pl.when(step >= 2)
-    def _():
-        for copy in stores(0, slot):
-            copy.wait()
-
+    for k in range(2):
+        keep(1, k).start()
     out_tile = min(256, width)
 
     def width_step(j, carry):
         cols = pl.ds(pl.multiple_of(j * out_tile, out_tile), out_tile)
         row_grad = dot_nn(mixed_ref[:, :hidden], gate_ref[:, cols])
         row_grad = row_grad + dot_nn(mixed_ref[:, hidden : 2 * hidden], up_ref[:, cols])
-        row_grad = row_grad + dot_nt(mixed_ref[:, 2 * hidden :], router_ref[cols, :])
-        rb[slot, :, cols] = row_grad.astype(jnp.bfloat16)
-        ob[slot, :, cols] = dot_nn(act_ref[...], down_ref[:, cols]).astype(jnp.bfloat16)
+        row_grad = row_grad + dot_nn(mixed_ref[:, 2 * hidden :], router_ref[:, cols])
+        row_grad = row_grad.astype(jnp.bfloat16)
+        out = dot_nn(act_ref[...], down_ref[:, cols]).astype(jnp.bfloat16)
+        for k in range(2):
+            row_refs[k][0, :, cols] = row_grad[k * rows : (k + 1) * rows]
+            out_refs[k][0, :, cols] = out[k * rows : (k + 1) * rows]
         return carry
 
     lax.fori_loop(0, width // out_tile, width_step, 0)
-    for j in range(pair_count):
-        @pl.when(step == j)
-        def _(j=j):
-            for copy in stores(2 * j, slot):
-                copy.start()
-
-    @pl.when(step == pair_count - 1)
-    def _():
-        for copy in stores(0, slot):
-            copy.wait()
-        if pair_count > 1:
-            for copy in stores(0, 1 - slot):
-                copy.wait()
-
-
-def expert_call(xs, cs, code, router, gate_mat, up_mat, down_mat, local_experts):
-    count = len(xs)
-    pair_count = count // 2
-    rows, width = xs[0].shape
+    for which in range(3):
+        for k in range(2):
+            keep(which, k).wait()
+
+
+def expert_call(where, xs, cotangents, codes, router, gate_mat, up_mat, down_mat, local_experts, kept):
+    chips, rows, width = xs[0].shape
     hidden = gate_mat.shape[0]
-    lane_pad = router.shape[1]
-    span = 2 * rows
+    lane_pad = router.shape[0]
     mixed_width = 2 * hidden + lane_pad
+    blocks = cotangents.shape[:2]
     any_spec = pl.BlockSpec(memory_space=pl.ANY)
-    whole = lambda shape: pl.BlockSpec(shape, lambda i: (0, 0), pipeline_mode=pl.Buffered(1))
-    block = jax.ShapeDtypeStruct((rows, width), jnp.bfloat16)
-    flops = 2 * span * pair_count * (width * hidden * 6 + width * lane_pad * 2)
+    whole = lambda shape: pl.BlockSpec(shape, lambda i, w: (0, 0), pipeline_mode=pl.Buffered(1))
+    near = lambda: pl.BlockSpec((1, rows, width), lambda i, w: (i, 0, 0))
+    mine = lambda last: pl.BlockSpec((1, 1, rows, last), lambda i, w: (2 * i + w[0], w[1], 0, 0))
+    theirs = lambda last: pl.BlockSpec((1, 1, rows, last), lambda i, w: (2 * i + 1 - w[0], w[1], 0, 0))
+    squeezed = lambda build: pl.BlockSpec((1, None, rows, width), build(width).index_map)
+    term = jax.ShapeDtypeStruct((chips, rows, width), jnp.bfloat16)
+    alls = [jax.ShapeDtypeStruct((*blocks, rows, last), jnp.bfloat16) for last in (width, mixed_width, hidden)]
+    count = 2 * chips * rows
     results = pl.pallas_call(
-        functools.partial(expert_kernel, pair_count, local_experts, lane_pad),
-        grid=(pair_count,),
-        out_shape=[block] * (2 * count)
-        + [
-            jax.ShapeDtypeStruct((span * pair_count, mixed_width), jnp.bfloat16),
-            jax.ShapeDtypeStruct((span * pair_count, hidden), jnp.bfloat16),
-        ],
-        in_specs=[any_spec] * (2 * count)
-        + [
-            pl.BlockSpec((1, span, lane_pad), lambda i: (i, 0, 0)),
-            whole((width, lane_pad)),
-            whole((hidden, width)),
-            whole((hidden, width)),
-            whole((hidden, width)),
-        ],
-        out_specs=[any_spec] * (2 * count)
-        + [
-            pl.BlockSpec((span, mixed_width), lambda i: (i, 0)),
-            pl.BlockSpec((span, hidden), lambda i: (i, 0)),
-        ],
-        scratch_shapes=[
-            pltpu.VMEM((2, span, width), jnp.bfloat16),
-            pltpu.VMEM((2, span, width), jnp.bfloat16),
-            pltpu.VMEM((2, span, width), jnp.bfloat16),
-            pltpu.VMEM((2, span, width), jnp.bfloat16),
-            pltpu.VMEM((span, hidden), jnp.bfloat16),
-            pltpu.SemaphoreType.DMA((2, 4)),
-            pltpu.SemaphoreType.DMA((2, 4)),
-        ],
+        functools.partial(expert_kernel, local_experts, len(kept)),
+        grid_spec=pltpu.PrefetchScalarGridSpec(
+            num_scalar_prefetch=1,
+            grid=(chips,),
+            in_specs=[near(), near(), squeezed(mine), squeezed(theirs), mine(lane_pad), theirs(lane_pad)]
+            + [whole((lane_pad, width))]
+            + [whole((hidden, width))] * 3
+            + [any_spec] * len(kept),
+            out_specs=[near() for _ in range(4)] + [any_spec] * 3,
+            scratch_shapes=[
+                pltpu.VMEM((2 * rows, mixed_width), jnp.bfloat16),
+                pltpu.VMEM((2 * rows, hidden), jnp.bfloat16),
+                pltpu.VMEM((2 * rows, hidden), jnp.bfloat16),
+                pltpu.SemaphoreType.DMA((3, 2)),
+            ],
+        ),
+        out_shape=[term] * 4 + alls,
+        input_output_aliases={11 + k: 4 + k for k in range(len(kept))},
         compiler_params=pltpu.CompilerParams(
             dimension_semantics=("arbitrary",), vmem_limit_bytes=60 * 1024 * 1024
         ),
         cost_estimate=pl.CostEstimate(
-            flops=flops,
-            bytes_accessed=count * rows * width * 8 + 6 * hidden * width,
-            transcendentals=span * pair_count * hidden,
+            flops=count * (12 * width * hidden + 4 * width * lane_pad),
+            bytes_accessed=count * (10 * width + 6 * hidden) + 6 * hidden * width,
+            transcendentals=count * hidden,
         ),
         name="experts",
-    )(*xs, *cs, code, router, gate_mat, up_mat, down_mat)
-    return results[:count], results[count : 2 * count], results[2 * count], results[2 * count + 1]
+    )(where, *xs, cotangents, cotangents, codes, codes, router, gate_mat, up_mat, down_mat, *kept)
+    return results[0:2], results[2:4], results[4:]
 
 
 def gathered(
@@ -844,39 +806,38 @@
     token_blocks = tp_gather(tokens)
     wide_shard = jnp.concatenate([query_weight, key_matrix, value_matrix], axis=1)
     wide_all = lax.all_gather(wide_shard, "fsdp", axis=0, tiled=True)
-    gains = lax.all_gather(
-        jnp.concatenate([first_gain, second_gain, query_gain, key_gain]), "fsdp", axis=0
-    )
-    gain_one = gains[:, : first_gain.shape[0]].reshape(-1).astype(full)
-    gains = gains[:, first_gain.shape[0] :]
-    gain_two = gains[:, : second_gain.shape[0]].reshape(-1).astype(full)
-    gains = gains[:, second_gain.shape[0] :]
-    gain_query = gains[:, : query_gain.shape[0]].reshape(-1).astype(full)
-    gain_key = gains[:, query_gain.shape[0] :].reshape(-1).astype(full)
-    router_all = lax.all_gather(router, "fsdp", axis=0, tiled=True)
-    output_all = lax.all_gather(output_weight, "fsdp", axis=0, tiled=True)
-
+
+    lane_pad = 128
     lanes = jnp.arange(expert_total, dtype=jnp.int32)
     picked = jnp.sum((expert_ids[:, :, None] == lanes[None, None, :]).astype(full), axis=1)
     order = jnp.arange(seq_len, dtype=jnp.int32)
     before = (order[None, :] < order[:, None]).astype(low)
     earlier = jnp.dot(before, picked.astype(low), preferred_element_type=full)
     code = (picked * (1.0 + (earlier < capacity).astype(full))).astype(low)
-    code = xor_order(code.reshape(tp_count, own_rows, expert_total), tp_rank, 0)
-    codes = jnp.swapaxes(code, 1, 2)[None]
-    for mask in (1, 2, 4):
-        codes = jnp.concatenate([codes, swap(codes, "fsdp", mask)], axis=0)
+    small_parts = [first_gain, second_gain, query_gain, key_gain, router.T, code.T]
+    small_shard = jnp.concatenate([part.reshape(-1) for part in small_parts])
+    small_size = small_shard.shape[0]
+    small_shard = jnp.pad(small_shard, (0, -small_size % (16 * lane_pad))).reshape(-1, lane_pad)
+    small_all = lax.all_gather(small_shard, "fsdp", axis=0).reshape(fsdp_count, -1)
+    taken = []
+    begin = 0
+    for part in small_parts:
+        taken.append(small_all[:, begin : begin + part.size])
+        begin += part.size
+    gain_one, gain_two, gain_query, gain_key = [part.reshape(-1).astype(full) for part in taken[:4]]
     shift = fsdp_rank * local_experts
-    codes = jnp.concatenate([codes, codes], axis=2)
-    codes = jnp.swapaxes(lax.dynamic_slice_in_dim(codes, shift, expert_total, 2), 2, 3)
-    lane_pad = 128
-    codes = jnp.pad(codes, ((0, 0), (0, 0), (0, 0), (0, lane_pad - expert_total)))
-    router_near = jnp.concatenate([router_all, router_all], axis=1)
-    router_near = lax.dynamic_slice_in_dim(router_near, shift, expert_total, 1)
-    router_near = jnp.pad(router_near, ((0, 0), (0, lane_pad - expert_total)))
-
-    cotangent_blocks = tp_gather(cotangent)
-    cotangent_near = [plane_gather(b, r % 2 == 1) for r, b in enumerate(cotangent_blocks)]
+    router_near = jnp.swapaxes(taken[4].reshape(fsdp_count, expert_total, -1), 0, 1).reshape(expert_total, model_dim)
+    router_near = lax.dynamic_slice_in_dim(
+        jnp.concatenate([router_near, router_near], axis=0), shift, expert_total, 0
+    )
+    router_near = jnp.pad(router_near, ((0, lane_pad - expert_total), (0, 0)))
+    codes = taken[5].reshape(fsdp_count, expert_total, seq_len)
+    codes = lax.dynamic_slice_in_dim(jnp.concatenate([codes, codes], axis=1), shift, expert_total, 1)
+    codes = jnp.pad(jnp.swapaxes(codes, 1, 2), ((0, 0), (0, 0), (0, lane_pad - expert_total)))
+    codes = codes.reshape(fsdp_count, tp_count, own_rows, lane_pad)
+    output_all = lax.all_gather(output_weight, "fsdp", axis=0, tiled=True)
+    cotangent_all = lax.all_gather(cotangent, ("fsdp", "tp"), axis=0, tiled=True)
+    cotangent_all = cotangent_all.reshape(fsdp_count, tp_count, own_rows, model_dim)
 
     segment_row = xor_order(segments[0].reshape(tp_count, own_rows), tp_rank, 0).reshape(-1)
     token_pos = xor_order(order.reshape(tp_count, own_rows), tp_rank, 0).reshape(-1)
@@ -912,30 +873,35 @@
     hidden_hat, hidden_inverse = norm_forward(hidden)
     normed_two = (hidden_hat * gain_two).astype(low)
 
-    normed_blocks = tp_gather(normed_two)
-    normed_near = [plane_gather(b, r % 2 == 1) for r, b in enumerate(normed_blocks)]
     gate_mat = gate_weight.reshape(-1, model_dim)
     up_mat = up_weight.reshape(-1, model_dim)
     down_mat = down_weight.reshape(-1, model_dim)
-    row_sums, out_sums, mixed_grads, act_gates = [], [], [], []
-    for r in range(tp_count):
-        code_r = codes[:, r].reshape(fsdp_count // 2, 2 * own_rows, lane_pad)
-        row_parts, out_parts, mixed_grad, act_gate = expert_call(
-            normed_near[r], cotangent_near[r], code_r, router_near, gate_mat, up_mat, down_mat, local_experts
+    core = fsdp_rank % 2
+    row_sums, out_terms, kept = [], [], ()
+    for r, block in enumerate(tp_gather(normed_two)):
+        near = plane_gather(block)
+        where = jnp.stack([core, tp_rank ^ r]).astype(jnp.int32)
+        row_terms, out_term, kept = expert_call(
+            where,
+            (near, swap(near, "fsdp", 1)),
+            cotangent_all,
+            codes,
+            router_near,
+            gate_mat,
+            up_mat,
+            down_mat,
+            local_experts,
+            kept,
         )
-        row_sums.append(plane_reduce(row_parts, r % 2 == 1))
-        out_sums.append(plane_reduce(out_parts, r % 2 == 1))
-        mixed_grads.append(mixed_grad)
-        act_gates.append(act_gate)
+        row_sums.append(plane_reduce(row_terms))
+        out_terms.append(out_term)
     normed_two_grad = tp_reduce(row_sums)
-    output = (hidden + tp_reduce(out_sums)).astype(low)
-
-    flat = lambda near: jnp.concatenate([b for blocks in near for b in blocks], axis=0)
-    wide_grad = jnp.einsum(
-        "tf,td->fd", jnp.concatenate(mixed_grads, axis=0), flat(normed_near), preferred_element_type=full
-    )
+    out_terms, normed_two_grad = lax.optimization_barrier((out_terms, normed_two_grad))
+    output = (hidden + tp_reduce([plane_reduce(term) for term in out_terms])).astype(low)
+    normed_all, mixed_all, act_all = [part.reshape(-1, part.shape[-1]) for part in kept]
+    wide_grad = jnp.einsum("tf,td->fd", mixed_all, normed_all, preferred_element_type=full)
     down_grad = jnp.einsum(
-        "tf,td->fd", jnp.concatenate(act_gates, axis=0), flat(cotangent_near), preferred_element_type=full
+        "tf,td->fd", act_all, cotangent_all.reshape(-1, model_dim), preferred_element_type=full
     )
     flat_hidden = local_experts * hidden_units
     gate_wgrad = wide_grad[:flat_hidden].reshape(gate_weight.shape)

time: 1860 us -> 1710 us (0.919)
  waiting for transfers between devices: 819 us -> 564 us
  starting transfers between devices: 112 us -> 243 us
  other arithmetic: 120 us -> 216 us
  local copies, waits for them, and re-layouts: 224 us -> 137 us
  blocking collectives: 35.5 us -> 13.3 us
    ppermute x144 -> x38, waiting for transfers between devices: 819 us -> 408 us  [swap(): return lax.ppermute(values, axis, partners(lax.axis_size(axis), mask))]
    all_to_all x0 -> x12, waiting for transfers between devices: none -> 155 us  [exchange(): lax.all_to_all(parts, 'fsdp', split_axis=0, concat_axis=0, tiled=True, ax...]
    unnamed x414 -> x213, local copies, waits for them, and re-layouts: 130 us -> 13.7 us
    ppermute x144 -> x38, starting transfers between devices: 112 us -> 183 us  [swap(): return lax.ppermute(values, axis, partners(lax.axis_size(axis), mask))]
    all_to_all x0 -> x12, starting transfers between devices: none -> 59.8 us  [exchange(): lax.all_to_all(parts, 'fsdp', split_axis=0, concat_axis=0, tiled=True, ax...]
    convert_element_type x31 -> x10, other arithmetic: 18.3 us -> 60.9 us  [the longest x8 60.6 us: plane_reduce(): both = add_low(terms[0], swap(terms[1], 'fsdp', 1)).astype(low)]
    reduce_sum x0 -> x8, other arithmetic: none -> 32.9 us  [plane_reduce(): return jnp.sum(exchange(both).astype(jnp.float32), axis=0).astype(low)]
    unnamed x1 -> x0, blocking collectives: 26 us -> none
  transfers between devices with their start and end apart: 148 -> 55, of which waited for: 51 -> 17; matrix products, arithmetic and copies ran while one was open for 30% -> 34% of each run, Pallas kernels for 15% -> 16%
where the time goes in v2:
time: 1710 us
  waiting for transfers between devices  564 us (33%)
  Pallas kernels  269 us (16%)
  starting transfers between devices  243 us (14%)
  matrix products  239 us (14%)
  other arithmetic  216 us (13%)
  local copies, waits for them, and re-layouts  137 us (8%)
    ppermute x38, waiting for transfers between devices, swap(): return lax.ppermute(values, axis, partners(lax.axis_size(axis), mask))  408 us
    pallas_call x4, Pallas kernels, expert_call(): pl.pallas_call(functools.partial(expert_kernel, local_experts, len(kept))...  269 us
    ppermute x38, starting transfers between devices, swap(): return lax.ppermute(values, axis, partners(lax.axis_size(axis), mask))  183 us
    all_to_all x12, waiting for transfers between devices, exchange(): lax.all_to_all(parts, 'fsdp', split_axis=0, concat_axis=0, tiled=True, ax...  155 us
    dot_general x1, matrix products, gathered(): jnp.einsum('tf,td->fd', mixed_all, normed_all, preferred_element_type=full)  67.7 us
    convert_element_type x8, other arithmetic, plane_reduce(): both = add_low(terms[0], swap(terms[1], 'fsdp', 1)).astype(low)  60.6 us
    all_to_all x12, starting transfers between devices, exchange(): lax.all_to_all(parts, 'fsdp', split_axis=0, concat_axis=0, tiled=True, ax...  59.8 us
  transfers between devices with their start and end apart: 55, of which 17 were waited for; matrix products, arithmetic and copies ran while one was open for 34% of the time, Pallas kernels for 16%

profile of v2, /device:TPU:0, one launch (start us, length us, event | category | flops | bytes accessed | tf_op | source)
XLA Modules:
  0.0 1707.1 jit_solution(1768831878896002623)
XLA Ops:
  59.0 27.1 %collective-permute-done.1 = bf16[256,2048]{1,0:T(8,128)(2,1)} collective-permute-done((bf16[256,2048]{1,0:T(8,128)(2,1)}, bf16[256,2048]{1,0:T(8,128)(2,1)}, u32[]{:S(2)}, u32[]{:S(2)}) %collective-permute-start.1) | collective-permute-done | bytes 1048608 | tf_op jit(solution)/shard_map/ppermute | solution.py:564
  117.6 42.2 %while.27 = (s32[]{:T(128)}, bf16[2,512,1024]{2,1,0:T(8,128)(2,1)}, f32[2,1,8,512]{3,2,1,0:T(8,128)S(1)}, s32[2]{0:T(128)S(1)}, s32[1024]{0:T(1024)S(1)}, /*inde...) while((s32[]{:T(128)}, bf16[2,512,1024]{2,1,0:T(8,128)(2,1)}, ...), condition=%wide.region_8.9_spmd, body=%wide.region_5.8_spmd.sunk | while | flops 2195715072 | bytes 59419340 | solution.py:863
  168.4 22.0 %collective-permute-start.3 = (bf16[256,2048]{1,0:T(8,128)(2,1)S(1)}, bf16[256,2048]{1,0:T(8,128)(2,1)S(1)}, u32[]{:S(2)}, u32[]{:S(2)}) collective-permute-start(bf16[256,2048]{1,0:T(8,128)(2,1)S(1)} %get-tuple-element.541), channel_id=1, source_target_pairs={{0,1},{1,0},{2,3},{3,2},{4,5},{5,4},{6,7},{7,6},{8,9},{9,8},{10,11... | collective-permute-start | bytes 3145736 | tf_op jit(solution)/shard_map/ppermute | solution.py:564
  192.9 81.9 %collective-permute-done.3 = bf16[256,2048]{1,0:T(8,128)(2,1)S(1)} collective-permute-done((bf16[256,2048]{1,0:T(8,128)(2,1)S(1)}, bf16[256,2048]{1,0:T(8,128)(2,1)S(1)}, u32[]{:S(2)}, u32[]{:S(2)}) %collective-permute-start.3) | collective-permute-done | bytes 1048608 | tf_op jit(solution)/shard_map/ppermute | solution.py:564
  274.8 22.2 %collective-permute-done.4 = bf16[256,2048]{1,0:T(8,128)(2,1)S(1)} collective-permute-done((bf16[256,2048]{1,0:T(8,128)(2,1)S(1)}, bf16[256,2048]{1,0:T(8,128)(2,1)S(1)}, u32[]{:S(2)}, u32[]{:S(2)}) %collective-permute-start.4) | collective-permute-done | bytes 1048608 | tf_op jit(solution)/shard_map/ppermute | solution.py:564
  297.0 27.3 %collective-permute-done.5 = bf16[256,2048]{1,0:T(8,128)(2,1)S(1)} collective-permute-done((bf16[256,2048]{1,0:T(8,128)(2,1)S(1)}, bf16[256,2048]{1,0:T(8,128)(2,1)S(1)}, u32[]{:S(2)}, u32[]{:S(2)}) %collective-permute-start.5) | collective-permute-done | bytes 1048608 | tf_op jit(solution)/shard_map/ppermute | solution.py:564
  335.1 47.4 %collective-permute-start.7 = (bf16[256,2048]{1,0:T(8,128)(2,1)S(1)}, bf16[256,2048]{1,0:T(8,128)(2,1)S(1)}, u32[]{:S(2)}, u32[]{:S(2)}) collective-permute-start(bf16[256,2048]{1,0:T(8,128)(2,1)S(1)} %multiply_convert_fusion), channel_id=1, source_target_pairs={{0,1},{1,0},{2,3},{3,2},{4,5},{5,4},{6,7},{7,6},{8,9},{9,8},{10,11... | collective-permute-start | bytes 3145736 | tf_op jit(solution)/shard_map/ppermute | solution.py:564
  406.3 26.4 %collective-permute-start.9 = (bf16[256,2048]{1,0:T(8,128)(2,1)S(1)}, bf16[256,2048]{1,0:T(8,128)(2,1)S(1)}, u32[]{:S(2)}, u32[]{:S(2)}) collective-permute-start(bf16[256,2048]{1,0:T(8,128)(2,1)S(1)} %multiply_convert_fusion), channel_id=1, source_target_pairs={{0,2},{1,3},{2,0},{3,1},{4,6},{5,7},{6,4},{7,5},{8,10},{9,11},{10,... | collective-permute-start | bytes 3145736 | tf_op jit(solution)/shard_map/ppermute | solution.py:564
  432.8 44.9 %collective-permute-done.9 = bf16[256,2048]{1,0:T(8,128)(2,1)S(1)} collective-permute-done((bf16[256,2048]{1,0:T(8,128)(2,1)S(1)}, bf16[256,2048]{1,0:T(8,128)(2,1)S(1)}, u32[]{:S(2)}, u32[]{:S(2)}) %collective-permute-start.9) | collective-permute-done | bytes 1048608 | tf_op jit(solution)/shard_map/ppermute | solution.py:564
  541.8 67.2 %experts.4 = (bf16[4,256,2048]{2,1,0:T(8,128)(2,1)}, bf16[4,256,2048]{2,1,0:T(8,128)(2,1)}, bf16[4,256,2048]{2,1,0:T(8,128)(2,1)}, bf16[4,256,2048]{2,1,0:T(8,12...) custom-call(s32[2]{0:T(128)} %pad_add_fusion.where_ref, ...), custom_call_target="tpu_custom_call" | custom-call | flops 40802189312 | bytes 60817408 | tf_op jit(solution)/shard_map/experts/pallas_call | solution.py:738
  609.0 67.2 %experts.5 = (bf16[4,256,2048]{2,1,0:T(8,128)(2,1)}, bf16[4,256,2048]{2,1,0:T(8,128)(2,1)}, bf16[4,256,2048]{2,1,0:T(8,128)(2,1)}, bf16[4,256,2048]{2,1,0:T(8,12...) custom-call(s32[2]{0:T(128)} %pad_add_fusion.1.where_ref, ...), custom_call_target="tpu_custom_call", output_to_operand_aliasing={{4}: (11, {}), {5}: (12, {}), {6}: (13, {})} | custom-call | flops 40802189312 | bytes 60817408 | tf_op jit(solution)/shard_map/experts/pallas_call | solution.py:738
  678.0 67.4 %experts.6 = (bf16[4,256,2048]{2,1,0:T(8,128)(2,1)}, bf16[4,256,2048]{2,1,0:T(8,128)(2,1)}, bf16[4,256,2048]{2,1,0:T(8,128)(2,1)}, bf16[4,256,2048]{2,1,0:T(8,12...) custom-call(s32[2]{0:T(128)} %pad_add_fusion.2.where_ref, ...), custom_call_target="tpu_custom_call", output_to_operand_aliasing={{4}: (11, {}), {5}: (12, {}), {6}: (13, {})} | custom-call | flops 40802189312 | bytes 60817408 | tf_op jit(solution)/shard_map/experts/pallas_call | solution.py:738
  758.5 67.4 %experts.7 = (bf16[4,256,2048]{2,1,0:T(8,128)(2,1)}, bf16[4,256,2048]{2,1,0:T(8,128)(2,1)}, bf16[4,256,2048]{2,1,0:T(8,128)(2,1)}, bf16[4,256,2048]{2,1,0:T(8,12...) custom-call(s32[2]{0:T(128)} %pad_add_fusion.3.where_ref, ...), custom_call_target="tpu_custom_call", output_to_operand_aliasing={{4}: (11, {}), {5}: (12, {}), {6}: (13, {})} | custom-call | flops 40802189312 | bytes 60817408 | tf_op jit(solution)/shard_map/experts/pallas_call | solution.py:738
  847.0 40.3 %all-to-all-done.6 = bf16[4,256,2048]{2,1,0:T(8,128)(2,1)} async-done(((bf16[4,256,2048]{2,1,0:T(8,128)(2,1)}), bf16[4,256,2048]{2,1,0:T(8,128)(2,1)}, u32[]{:S(2)}, u32[]{:S(2)}) %all-to-all-start.6) | async-done | bytes 4194336 | tf_op jit(solution)/shard_map/all_to_all | solution.py:585
  899.9 40.0 %all-to-all-done.7 = bf16[4,256,2048]{2,1,0:T(8,128)(2,1)} async-done(((bf16[4,256,2048]{2,1,0:T(8,128)(2,1)}), bf16[4,256,2048]{2,1,0:T(8,128)(2,1)}, u32[]{:S(2)}, u32[]{:S(2)}) %all-to-all-start.7) | async-done | bytes 4194336 | tf_op jit(solution)/shard_map/all_to_all | solution.py:585
  966.4 25.6 %all-to-all-done.4 = bf16[4,256,2048]{2,1,0:T(8,128)(2,1)} async-done(((bf16[4,256,2048]{2,1,0:T(8,128)(2,1)}), bf16[4,256,2048]{2,1,0:T(8,128)(2,1)}, u32[]{:S(2)}, u32[]{:S(2)}) %all-to-all-start.4) | async-done | bytes 4194336 | tf_op jit(solution)/shard_map/all_to_all | solution.py:585
  995.2 30.6 %collective-permute-done.17 = bf16[256,2048]{1,0:T(8,128)(2,1)S(1)} collective-permute-done((bf16[256,2048]{1,0:T(8,128)(2,1)}, bf16[256,2048]{1,0:T(8,128)(2,1)S(1)}, u32[]{:S(2)}, u32[]{:S(2)}) %collective-permute-start.17) | collective-permute-done | bytes 1048608 | tf_op jit(solution)/shard_map/ppermute | solution.py:564
  1052.9 67.7 %convolution_bitcast_fusion.1 = f32[1664,2048]{1,0:T(8,128)S(1)} fusion(bf16[8,4,256,1664]{3,2,1,0:T(8,128)(2,1)} %get-tuple-element.232, bf16[8,4,256,2048]{3,2,1,0:T(8,128)(2,1)} %get-tuple-element.233), kind=kOutput, calls=%fused_computation.55 | convolution fusion | flops 55834574848 | bytes 74448896 | tf_op jit(solution)/shard_map/tf,td->fd/dot_general | solution.py:902
  1147.1 98.0 %while.28 = (s32[]{:T(128)}, f32[1024,1,128]{0,2,1:T(8,128)}, f32[1024,1,128]{0,2,1:T(8,128)}, f32[2,512,8,128]{3,2,1,0:T(8,128)}, s32[2]{0:T(128)S(1)}, /*index...) while((s32[]{:T(128)}, f32[1024,1,128]{0,2,1:T(8,128)}, ...), condition=%wide.region_22.23_spmd.clone, body=%wide.region_20.22_spmd.clone.sunk | while | flops 5409731584 | bytes 187689904 | solution.py:920
  1360.4 30.5 %collective-permute-done.31 = bf16[256,2048]{1,0:T(8,128)(2,1)S(1)} collective-permute-done((bf16[256,2048]{1,0:T(8,128)(2,1)}, bf16[256,2048]{1,0:T(8,128)(2,1)S(1)}, u32[]{:S(2)}, u32[]{:S(2)}) %collective-permute-start.31) | collective-permute-done | bytes 1048608 | tf_op jit(solution)/shard_map/ppermute | solution.py:564
  1484.0 28.0 %all-to-all-done.11 = bf16[4,256,2048]{2,1,0:T(8,128)(2,1)} async-done(((bf16[4,256,2048]{2,1,0:T(8,128)(2,1)}), bf16[4,256,2048]{2,1,0:T(8,128)(2,1)}, u32[]{:S(2)}, u32[]{:S(2)}) %all-to-all-start.11) | async-done | bytes 4194336 | tf_op jit(solution)/shard_map/all_to_all | solution.py:585
  1517.2 33.7 %fusion.38 = f32[4,192,2048]{2,1,0:T(8,128)} fusion(bf16[4,192,8192]{2,1,0:T(8,128)(2,1)} %bitcast.468, bf16[8192,2048]{1,0:T(8,128)(2,1)} %all-gather.8.cloned.1.call-done), kind=kOutput, calls=%fused_computation.51 | convolution fusion | flops 25769803776 | bytes 52428800 | tf_op jit(solution)/shard_map/tf,td->fd/dot_general | solution.py:903
  1550.9 31.9 %collective-permute-start.36 = (f32[2,2184]{1,0:T(2,128)S(1)}, f32[2,2184]{1,0:T(2,128)S(1)}, u32[]{:S(2)}, u32[]{:S(2)}) collective-permute-start(f32[2,2184]{1,0:T(2,128)S(1)} %slice.172), channel_id=1, source_target_pairs={{0,1},{1,0},{2,3},{3,2},{4,5},{5,4},{6,7},{7,6},{8,9},{9,8},{10,11... | collective-permute-start | bytes 52424 | tf_op jit(solution)/shard_map/ppermute | solution.py:564
  1611.8 69.6 %collective-permute-done.37 = f32[2184]{0:T(1024)S(1)} collective-permute-done((f32[2184]{0:T(1024)S(1)}, f32[2184]{0:T(1024)S(1)}, u32[]{:S(2)}, u32[]{:S(2)}) %collective-permute-start.37) | collective-permute-done | bytes 8768 | tf_op jit(solution)/shard_map/ppermute | solution.py:564
  (600 shorter events, 716.1 us)
Async XLA Ops:
  7.2 82.2 %all-gather.4.cloned.1.call-start = ((), (), s32[]{:S(2)}) async-start(), calls=%async_computation.14 | async-start | bytes 5898240 | tf_op jit(solution)/shard_map/all_gather | solution.py:808
  9.3 150.6 %all-gather.6.cloned.1.call-start = ((), (), s32[]{:S(2)}) async-start(), calls=%async_computation.15 | async-start | bytes 4718592 | tf_op jit(solution)/shard_map/all_gather | solution.py:838
  10.1 531.7 %all-gather.8.cloned.1.call-start = ((), (), s32[]{:S(2)}) async-start(), calls=%async_computation.16 | async-start | bytes 34603008 | tf_op jit(solution)/shard_map/all_gather | solution.py:839
  168.4 106.4 %collective-permute-start.3 = (bf16[256,2048]{1,0:T(8,128)(2,1)S(1)}, bf16[256,2048]{1,0:T(8,128)(2,1)S(1)}, u32[]{:S(2)}, u32[]{:S(2)}) collective-permute-start(bf16[256,2048]{1,0:T(8,128)(2,1)S(1)} %get-tuple-element.541), channel_id=1, source_target_pairs={{0,1},{1,0},{2,3},{3,2},{4,5},{5,4},{6,7},{7,6},{8,9},{9,8},{10,11... | collective-permute-start | bytes 3145736 | tf_op jit(solution)/shard_map/ppermute | solution.py:564
  190.4 106.6 %collective-permute-start.4 = (bf16[256,2048]{1,0:T(8,128)(2,1)S(1)}, bf16[256,2048]{1,0:T(8,128)(2,1)S(1)}, u32[]{:S(2)}, u32[]{:S(2)}) collective-permute-start(bf16[256,2048]{1,0:T(8,128)(2,1)S(1)} %get-tuple-element.543), channel_id=1, source_target_pairs={{0,2},{1,3},{2,0},{3,1},{4,6},{5,7},{6,4},{7,5},{8,10},{9,11},{10,... | collective-permute-start | bytes 3145736 | tf_op jit(solution)/shard_map/ppermute | solution.py:564
  191.5 132.8 %collective-permute-start.5 = (bf16[256,2048]{1,0:T(8,128)(2,1)S(1)}, bf16[256,2048]{1,0:T(8,128)(2,1)S(1)}, u32[]{:S(2)}, u32[]{:S(2)}) collective-permute-start(bf16[256,2048]{1,0:T(8,128)(2,1)S(1)} %get-tuple-element.542), channel_id=1, source_target_pairs={{0,3},{1,2},{2,1},{3,0},{4,7},{5,6},{6,5},{7,4},{8,11},{9,10},{10,... | collective-permute-start | bytes 3145736 | tf_op jit(solution)/shard_map/ppermute | solution.py:564
  432.7 109.0 %collective-permute-start.6 = (bf16[4,256,2048]{2,1,0:T(8,128)(2,1)}, bf16[4,256,2048]{2,1,0:T(8,128)(2,1)}, u32[]{:S(2)}, u32[]{:S(2)}) collective-permute-start(bf16[4,256,2048]{2,1,0:T(8,128)(2,1)} %all-to-all-done.refs_0_), channel_id=1, source_target_pairs={{0,4},{4,0},{8,12},{12,8},{16,20},{20,16},{24,28},{28,24},{1,5},{5... | collective-permute-start | bytes 12582920 | tf_op jit(solution)/shard_map/ppermute | solution.py:564
  492.7 116.3 %collective-permute-start.8 = (bf16[4,256,2048]{2,1,0:T(8,128)(2,1)}, bf16[4,256,2048]{2,1,0:T(8,128)(2,1)}, u32[]{:S(2)}, u32[]{:S(2)}) collective-permute-start(bf16[4,256,2048]{2,1,0:T(8,128)(2,1)} %all-to-all-done.1.refs_0_), channel_id=1, source_target_pairs={{0,4},{4,0},{8,12},{12,8},{16,20},{20,16},{24,28},{28,24},{1,5},{5... | collective-permute-start | bytes 12582920 | tf_op jit(solution)/shard_map/ppermute | solution.py:564
  536.7 141.3 %all-to-all-start.3 = ((bf16[4,256,2048]{2,1,0:T(8,128)(2,1)}), bf16[4,256,2048]{2,1,0:T(8,128)(2,1)}, u32[]{:S(2)}, u32[]{:S(2)}) async-start(bf16[4,256,2048]{2,1,0:T(8,128)(2,1)} %broadcast_in_dim.55), calls=%async_computation.3 | async-start | bytes 8388608 | tf_op jit(solution)/shard_map/all_to_all | solution.py:585
  541.7 136.3 %collective-permute-start.10 = (bf16[4,256,2048]{2,1,0:T(8,128)(2,1)}, bf16[4,256,2048]{2,1,0:T(8,128)(2,1)}, u32[]{:S(2)}, u32[]{:S(2)}) collective-permute-start(bf16[4,256,2048]{2,1,0:T(8,128)(2,1)} %all-to-all-done.2.refs_0_), channel_id=1, source_target_pairs={{0,4},{4,0},{8,12},{12,8},{16,20},{20,16},{24,28},{28,24},{1,5},{5... | collective-permute-start | bytes 12582920 | tf_op jit(solution)/shard_map/ppermute | solution.py:564
  745.4 80.6 %collective-permute-start.16 = (bf16[4,256,2048]{2,1,0:T(8,128)(2,1)}, bf16[4,256,2048]{2,1,0:T(8,128)(2,1)}, u32[]{:S(2)}, u32[]{:S(2)}) collective-permute-start(bf16[4,256,2048]{2,1,0:T(8,128)(2,1)} %get-tuple-element.216), channel_id=1, source_target_pairs={{0,4},{4,0},{8,12},{12,8},{16,20},{20,16},{24,28},{28,24},{1,5},{5... | collective-permute-start | bytes 12582920 | tf_op jit(solution)/shard_map/ppermute | solution.py:564
  1029.1 109.0 %collective-permute-start.27 = (bf16[256,2048]{1,0:T(8,128)(2,1)S(1)}, bf16[256,2048]{1,0:T(8,128)(2,1)S(1)}, u32[]{:S(2)}, u32[]{:S(2)}) collective-permute-start(bf16[256,2048]{1,0:T(8,128)(2,1)S(1)} %fusion.97), channel_id=1, source_target_pairs={{0,1},{1,0},{2,3},{3,2},{4,5},{5,4},{6,7},{7,6},{8,9},{9,8},{10,11... | collective-permute-start | bytes 3145736 | tf_op jit(solution)/shard_map/ppermute | solution.py:564
  1050.4 87.7 %collective-permute-start.28 = (bf16[256,2048]{1,0:T(8,128)(2,1)S(1)}, bf16[256,2048]{1,0:T(8,128)(2,1)}, u32[]{:S(2)}, u32[]{:S(2)}) collective-permute-start(bf16[256,2048]{1,0:T(8,128)(2,1)S(1)} %fusion.97), channel_id=1, source_target_pairs={{0,2},{1,3},{2,0},{3,1},{4,6},{5,7},{6,4},{7,5},{8,10},{9,11},{10,... | collective-permute-start | bytes 3145736 | tf_op jit(solution)/shard_map/ppermute | solution.py:564
  1051.3 86.8 %collective-permute-start.29 = (bf16[256,2048]{1,0:T(8,128)(2,1)S(1)}, bf16[256,2048]{1,0:T(8,128)(2,1)}, u32[]{:S(2)}, u32[]{:S(2)}) collective-permute-start(bf16[256,2048]{1,0:T(8,128)(2,1)S(1)} %fusion.97), channel_id=1, source_target_pairs={{0,3},{1,2},{2,1},{3,0},{4,7},{5,6},{6,5},{7,4},{8,11},{9,10},{10,... | collective-permute-start | bytes 3145736 | tf_op jit(solution)/shard_map/ppermute | solution.py:564
  1137.4 182.0 %collective-permute-start.21 = (bf16[4,256,2048]{2,1,0:T(8,128)(2,1)}, bf16[4,256,2048]{2,1,0:T(8,128)(2,1)}, u32[]{:S(2)}, u32[]{:S(2)}) collective-permute-start(bf16[4,256,2048]{2,1,0:T(8,128)(2,1)} %get-tuple-element.222), channel_id=1, source_target_pairs={{0,4},{4,0},{8,12},{12,8},{16,20},{20,16},{24,28},{28,24},{1,5},{5... | collective-permute-start | bytes 12582920 | tf_op jit(solution)/shard_map/ppermute | solution.py:564
  1137.5 264.9 %collective-permute-start.23 = (bf16[4,256,2048]{2,1,0:T(8,128)(2,1)}, bf16[4,256,2048]{2,1,0:T(8,128)(2,1)}, u32[]{:S(2)}, u32[]{:S(2)}) collective-permute-start(bf16[4,256,2048]{2,1,0:T(8,128)(2,1)} %get-tuple-element.224), channel_id=1, source_target_pairs={{0,4},{4,0},{8,12},{12,8},{16,20},{20,16},{24,28},{28,24},{1,5},{5... | collective-permute-start | bytes 12582920 | tf_op jit(solution)/shard_map/ppermute | solution.py:564
  1138.0 313.3 %collective-permute-start.25 = (bf16[4,256,2048]{2,1,0:T(8,128)(2,1)}, bf16[4,256,2048]{2,1,0:T(8,128)(2,1)}, u32[]{:S(2)}, u32[]{:S(2)}) collective-permute-start(bf16[4,256,2048]{2,1,0:T(8,128)(2,1)} %get-tuple-element.226), channel_id=1, source_target_pairs={{0,4},{4,0},{8,12},{12,8},{16,20},{20,16},{24,28},{28,24},{1,5},{5... | collective-permute-start | bytes 12582920 | tf_op jit(solution)/shard_map/ppermute | solution.py:564
  1327.4 82.9 %all-to-all-start.9 = ((bf16[4,256,2048]{2,1,0:T(8,128)(2,1)}), bf16[4,256,2048]{2,1,0:T(8,128)(2,1)}, u32[]{:S(2)}, u32[]{:S(2)}) async-start(bf16[4,256,2048]{2,1,0:T(8,128)(2,1)} %add_convert_fusion.2), calls=%async_computation.9 | async-start | bytes 8388608 | tf_op jit(solution)/shard_map/all_to_all | solution.py:585
  1332.4 351.0 %reduce-scatter.5.cloned.1.call-start = ((), (), s32[]{:S(2)}) async-start(), calls=%async_computation.18 | async-start | bytes 4718592 | tf_op jit(solution)/shard_map/reduce_scatter | solution.py:973
  1464.1 232.5 %reduce-scatter.3.cloned.1.call-start = ((), (), s32[]{:S(2)}) async-start(), calls=%async_computation.17 | async-start | bytes 5898240 | tf_op jit(solution)/shard_map/reduce_scatter | solution.py:972
  1512.1 173.5 %all-to-all-start.8 = ((bf16[4,256,2048]{2,1,0:T(8,128)(2,1)}), bf16[4,256,2048]{2,1,0:T(8,128)(2,1)}, u32[]{:S(2)}, u32[]{:S(2)}) async-start(bf16[4,256,2048]{2,1,0:T(8,128)(2,1)} %add_convert_fusion.3), calls=%async_computation.8 | async-start | bytes 8388608 | tf_op jit(solution)/shard_map/all_to_all | solution.py:585
  1587.1 102.8 %collective-permute-start.22 = (bf16[256,2048]{1,0:T(8,128)(2,1)}, bf16[256,2048]{1,0:T(8,128)(2,1)}, u32[]{:S(2)}, u32[]{:S(2)}) collective-permute-start(bf16[256,2048]{1,0:T(8,128)(2,1)} %reduce_sum.265), channel_id=1, source_target_pairs={{0,1},{1,0},{2,3},{3,2},{4,5},{5,4},{6,7},{7,6},{8,9},{9,8},{10,11... | collective-permute-start | bytes 3145736 | tf_op jit(solution)/shard_map/ppermute | solution.py:564
  1591.3 98.5 %collective-permute-start.24 = (bf16[256,2048]{1,0:T(8,128)(2,1)}, bf16[256,2048]{1,0:T(8,128)(2,1)}, u32[]{:S(2)}, u32[]{:S(2)}) collective-permute-start(bf16[256,2048]{1,0:T(8,128)(2,1)} %reduce_sum.266), channel_id=1, source_target_pairs={{0,2},{1,3},{2,0},{3,1},{4,6},{5,7},{6,4},{7,5},{8,10},{9,11},{10,... | collective-permute-start | bytes 3145736 | tf_op jit(solution)/shard_map/ppermute | solution.py:564
  1598.6 91.3 %collective-permute-start.26 = (bf16[256,2048]{1,0:T(8,128)(2,1)}, bf16[256,2048]{1,0:T(8,128)(2,1)}, u32[]{:S(2)}, u32[]{:S(2)}) collective-permute-start(bf16[256,2048]{1,0:T(8,128)(2,1)} %reduce_sum.267), channel_id=1, source_target_pairs={{0,3},{1,2},{2,1},{3,0},{4,7},{5,6},{6,5},{7,4},{8,11},{9,10},{10,... | collective-permute-start | bytes 3145736 | tf_op jit(solution)/shard_map/ppermute | solution.py:564
  (138 other events, 4178.4 us)
Sparse Core Ops, SparseCore 0:
  10.5 46.3 all-gather.3
  58.8 36.5 all-gather.5
  98.4 277.7 all-gather.7
  1342.1 60.9 reduce-scatter.4
  1473.5 111.0 reduce-scatter.2
